TPU v7x, 32 devices: a whole 2x2x4 slice. The times are simulated.
32 devices in a mesh: dp: 32 (over z, y, x, core).
Axes of the slice: x: 2, y: 2, z: 4, core: 2. Of those that a mesh axis runs over, the one named last changes fastest.
Arguments:
- tokens: bfloat16 [16384, 768], P('dp'), may hold values from -6 to 6
- cotangent: bfloat16 [16384, 768], P('dp'), may hold values from -15 to 15
- seq_lengths: int32 [32, 2], P('dp'), may hold values from 0 to 512, as said below
- random_feat: bfloat16 [12, 64, 64], replicated, may hold values from -4 to 4
- w_qkv: float32 [768, 2304], P('dp'), may hold values from -0.21875 to 0.21875
- b_qkv: float32 [2304], P('dp'), may hold values from -1.5 to 1.5
- w_out: float32 [768, 768], P('dp'), may hold values from -0.875 to 0.875
- b_out: float32 [768], P('dp'), may hold values from -1.5 to 1.5
- ln1_gain: float32 [768], P('dp'), may hold values from 0.25 to 1.75
- ln1_bias: float32 [768], P('dp'), may hold values from -1.5 to 1.5
- w_up: float32 [768, 3072], P('dp'), may hold values from -0.21875 to 0.21875
- b_up: float32 [3072], P('dp'), may hold values from -1.5 to 1.5
- w_down: float32 [3072, 768], P('dp'), may hold values from -0.109375 to 0.109375
- b_down: float32 [768], P('dp'), may hold values from -1.5 to 1.5
- ln2_gain: float32 [768], P('dp'), may hold values from 0.25 to 1.75
- ln2_bias: float32 [768], P('dp'), may hold values from -1.5 to 1.5
- rpe_table: float32 [12288], P('dp'), may hold values from -2.5 to 2.5
Outputs:
- out: bfloat16 [16384, 768], P('dp')
- grad_tokens: float32 [16384, 768], P('dp')
- grad_w_qkv: float32 [768, 2304], P('dp')
- grad_b_qkv: float32 [2304], P('dp')
- grad_w_out: float32 [768, 768], P('dp')
- grad_b_out: float32 [768], P('dp')
- grad_ln1_gain: float32 [768], P('dp')
- grad_ln1_bias: float32 [768], P('dp')
- grad_w_up: float32 [768, 3072], P('dp')
- grad_b_up: float32 [3072], P('dp')
- grad_w_down: float32 [3072, 768], P('dp')
- grad_b_down: float32 [768], P('dp')
- grad_ln2_gain: float32 [768], P('dp')
- grad_ln2_bias: float32 [768], P('dp')
- grad_rpe: float32 [12288], P('dp')
Inputs may be any that keep to these rules, and one draw needn't show every extreme that they name: `seq_lengths`: row n gives the lengths of the one or two sequences packed from the start of device n's 512 token slots; a second length of 0 means one sequence; the two lengths sum to 512 or less, and some row holds one sequence of exactly 512.
All inputs are finite; a program needn't handle non-finite values.
Results may differ from a plain program's by a relative error of at most 0.018.
Values may be sent and summed in bfloat16 or wider, within the bound.
A program may use at most 192 MiB of HBM per device.

v0:
```python
import functools

import jax
import jax.numpy as jnp
from jax import lax
from jax.experimental import pallas as pl
from jax.experimental.pallas import tpu as pltpu
from jax.sharding import PartitionSpec as P

EPSILON = 1e-05
F32 = jnp.float32
LOW = jnp.bfloat16
MESH = pl.DeviceIdType.MESH
MIB = 2**20


def mm(first_op, second_op, first_dim=1, second_dim=0):
    return lax.dot_general(
        first_op,
        second_op,
        (((first_dim,), (second_dim,)), ((), ())),
        preferred_element_type=F32,
    )


def mm2(value, weight, weight_dim=0):
    high = value.astype(LOW)
    rest = (value - high.astype(F32)).astype(LOW)
    return mm(high, weight, 1, weight_dim) + mm(rest, weight, 1, weight_dim)


def iota(shape, dim):
    return lax.broadcasted_iota(jnp.int32, shape, dim)


def cols(index, width):
    return pl.ds(pl.multiple_of(index * width, width), width)


def build_tables(seq_ref, feat_ref, mask_ref, block_ref, ones_ref):
    rows = mask_ref.shape[0]
    first_end = seq_ref[0, 0]
    second_end = first_end + seq_ref[0, 1]

    def segment(place):
        return (place >= first_end).astype(jnp.int32) + (place >= second_end).astype(jnp.int32)

    across = segment(iota((128, rows), 1))
    for start in range(0, rows, 128):
        down = segment(iota((128, rows), 0) + start)
        mask_ref[start : start + 128, :] = jnp.where(down == across, 1.0, 0.0)
    head_size = feat_ref.shape[1]
    breadth = ones_ref.shape[0]
    group = breadth // head_size
    bits = head_size.bit_length() - 1
    owner_row = lax.shift_right_logical(iota((breadth, breadth), 0), bits)
    owner_col = lax.shift_right_logical(iota((breadth, breadth), 1), bits)
    same = owner_row == owner_col
    ones_ref[...] = jnp.where(same, 1.0, 0.0).astype(LOW)
    for index in range(feat_ref.shape[0] // group):
        rows_of = []
        for inner in range(group):
            piece = feat_ref[index * group + inner].astype(F32)
            rows_of.append(jnp.concatenate([piece] * group, axis=1))
        full = jnp.concatenate(rows_of, axis=0)
        block_ref[index] = jnp.where(same, full, 0.0).astype(LOW)


def project(tokens_ref, w_ref, vec_ref, scaled_ref, phi_ref, low_ref, block_ref, ones_ref):
    breadth = tokens_ref.shape[1]
    tile = ones_ref.shape[0]
    per_part = breadth // tile
    scale = 64 ** (-0.25)

    def features(step, carry):
        where = cols(step, tile)
        acc = mm(tokens_ref[...], w_ref[:, where]) + vec_ref[0:1, where]
        scaled = acc * scale
        scaled_ref[:, where] = scaled
        block = block_ref[lax.rem(step, per_part)]
        mapped = mm2(scaled, block)
        squared = mm2(scaled * scaled, ones_ref[...])
        phi = jnp.exp(mapped - 0.5 * squared) * 0.125
        phi_ref[:, where] = phi
        low_ref[:, where] = phi.astype(LOW)
        return carry

    lax.fori_loop(0, 2 * per_part, features, 0)

    def plain(step, carry):
        where = cols(step + 2 * per_part, tile)
        acc = mm(tokens_ref[...], w_ref[:, where]) + vec_ref[0:1, where]
        low_ref[:, where] = acc.astype(LOW)
        return carry

    lax.fori_loop(0, per_part, plain, 0)


def coefficients(rpe_ref, head, coef_ref):
    flip = (iota((128, 128), 0) + iota((128, 128), 1) == 127).astype(F32).astype(LOW)
    raw = rpe_ref[pl.ds(pl.multiple_of(head * 8, 8), 8), :].astype(LOW)
    table = jnp.exp(mm(raw, flip))
    wide = jnp.concatenate(
        [jnp.broadcast_to(table[7 - k : 8 - k, :], (128, 128)) for k in range(8)], axis=1
    )
    coef_ref[...] = pltpu.roll(wide, 1024 - 127, axis=1, stride=1, stride_axis=0)


def attend(low_ref, rpe_ref, mask_ref, den_ref, ctx_ref, ctx_low_ref, coef_ref, key_ref):
    rows, breadth = ctx_ref.shape

    def pair_step(pair, carry):
        q_at = cols(pair, 128)
        k_at = pl.ds(pl.multiple_of(pair * 128 + breadth, 128), 128)
        v_at = pl.ds(pl.multiple_of(pair * 128 + 2 * breadth, 128), 128)
        lane = iota((128, 128), 1)
        for side in range(2):
            coefficients(rpe_ref, pair * 2 + side, coef_ref)
            mine = lane >= 64 if side else lane < 64
            keep_half(low_ref, k_at, key_ref, side)
            for block in range(rows // 128):
                at = slice(block * 128, block * 128 + 128)
                kernel = mm(low_ref[at, q_at], key_ref[...], 1, 1)
                lead = 128 * (rows // 128 - 1 - block)
                scores = kernel * (coef_ref[:, lead : lead + rows] * mask_ref[at, :])
                total = jnp.sum(scores, axis=1, keepdims=True)
                context = mm(scores.astype(LOW), low_ref[:, v_at]) * (1.0 / total)
                total = jnp.broadcast_to(total, (128, 128))
                if side == 0:
                    den_ref[at, q_at] = total
                    ctx_ref[at, q_at] = context
                else:
                    den_ref[at, q_at] = jnp.where(mine, total, den_ref[at, q_at])
                    context = jnp.where(mine, context, ctx_ref[at, q_at])
                    ctx_ref[at, q_at] = context
                    ctx_low_ref[at, q_at] = context.astype(LOW)
        return carry

    lax.fori_loop(0, breadth // 128, pair_step, 0)


def keep_half(low_ref, where, out_ref, side):
    rows = low_ref.shape[0]
    lane = iota((rows, 128), 1)
    mine = lane >= 64 if side else lane < 64
    out_ref[...] = jnp.where(mine, low_ref[:, where].astype(F32), 0.0).astype(LOW)


def forward_kernel(
    seq_ref, tokens_ref, feat_ref, w_ref, vec_ref, rpe_ref,
    scaled_ref, phi_ref, low_ref, den_ref, ctx_ref, ctx_low_ref,
    mask_ref, block_ref, ones_ref, coef_ref, key_ref,
):
    build_tables(seq_ref, feat_ref, mask_ref, block_ref, ones_ref)
    project(tokens_ref, w_ref, vec_ref, scaled_ref, phi_ref, low_ref, block_ref, ones_ref)
    attend(low_ref, rpe_ref, mask_ref, den_ref, ctx_ref, ctx_low_ref, coef_ref, key_ref)


def norm(value):
    centred = value - jnp.mean(value, axis=-1, keepdims=True)
    inverse = lax.rsqrt(jnp.mean(centred * centred, axis=-1, keepdims=True) + EPSILON)
    return centred * inverse, inverse


def norm_back(grad, xhat, inverse, gain):
    scaled = grad * gain
    mean = jnp.mean(scaled, axis=-1, keepdims=True)
    along = jnp.mean(scaled * xhat, axis=-1, keepdims=True)
    return inverse * (scaled - mean - xhat * along)


def add_to(ref, row, value):
    ref[row : row + 1, 0 : value.shape[1]] += value


def column_sum(value):
    return jnp.sum(value, axis=0, keepdims=True)


def middle_kernel(
    seq_ref, tokens_ref, cot_ref, ctx_low_ref, vec_ref, w_out_ref, w_up_ref, w_down_ref,
    out_ref, g_hidden_ref, g_ctx_ref, d_out_ref, d_up_ref, d_down_ref, gvec_ref,
    wide_ref, normed_ref, normed_low_ref, xhat_ref, inverse_ref, act_ref, slope_ref, g_sum_ref,
    g_low_ref, g_up_ref, flip_ref,
):
    rows, breadth = tokens_ref.shape
    hidden = w_up_ref.shape[1]
    height, tile = 128, 256
    blocks, tiles = rows // height, breadth // tile
    valid_rows = seq_ref[0, 0] + seq_ref[0, 1]
    gvec_ref[...] = jnp.zeros_like(gvec_ref)
    gain_one, bias_one = vec_ref[3:4, :breadth], vec_ref[4:5, :breadth]
    gain_two, bias_two = vec_ref[6:7, :breadth], vec_ref[7:8, :breadth]

    def rows_at(step):
        return pl.ds(pl.multiple_of(step * height, height), height)

    def loop(count, step):
        def run(index, carry):
            step(index)
            return carry

        lax.fori_loop(0, count, run, 0)

    def attended_step(step):
        where = cols(step, tile)
        wide_ref[:, where] = mm(ctx_low_ref[...], w_out_ref[:, where]) + vec_ref[2:3, where]

    loop(tiles, attended_step)

    def first_norm(step):
        at = rows_at(step)
        xhat, inverse = norm(tokens_ref[at, :].astype(F32) + wide_ref[at, :])
        xhat_ref[at, :] = xhat
        inverse_ref[at, :] = jnp.broadcast_to(inverse, (height, 128))
        normed = xhat * gain_one + bias_one
        normed_ref[at, :] = normed
        normed_low_ref[at, :] = normed.astype(LOW)

    loop(blocks, first_norm)

    def upward_step(step):
        where = cols(step, tile)
        upward = mm(normed_low_ref[...], w_up_ref[:, where]) + vec_ref[1:2, where]
        phi = 0.5 + 0.5 * lax.erf(upward * 0.5**0.5)
        density = jnp.exp(-0.5 * upward * upward) * 0.3989422804014327
        act_ref[:, where] = (upward * phi).astype(LOW)
        slope_ref[:, where] = phi + upward * density

    loop(hidden // tile, upward_step)

    def downward_step(step):
        where = cols(step, tile)
        wide_ref[:, where] = mm(act_ref[...], w_down_ref[:, where]) + vec_ref[5:6, where]

    loop(tiles, downward_step)

    def second_norm(step):
        at = rows_at(step)
        xhat, inverse = norm(normed_ref[at, :] + wide_ref[at, :])
        out_ref[at, :] = (xhat * gain_two + bias_two).astype(LOW)
        place = iota((height, breadth), 0) + step * height
        grad = jnp.where(place < valid_rows, cot_ref[at, :].astype(F32), 0.0)
        add_to(gvec_ref, 6, column_sum(grad * xhat))
        add_to(gvec_ref, 7, column_sum(grad))
        g_sum = norm_back(grad, xhat, inverse, gain_two)
        add_to(gvec_ref, 5, column_sum(g_sum))
        g_sum_ref[at, :] = g_sum
        g_low_ref[at, :] = g_sum.astype(LOW)

    loop(blocks, second_norm)
    flip_ref[...] = jnp.transpose(normed_low_ref[...])

    def down_step(step):
        where = cols(step, tile)
        g_upward = mm(g_low_ref[...], w_down_ref[where, :], 1, 1) * slope_ref[:, where]
        gvec_ref[1:2, where] = column_sum(g_upward)
        g_upward = g_upward.astype(LOW)
        g_up_ref[:, where] = g_upward
        d_down_ref[where, :] = mm(act_ref[:, where], g_low_ref[...], 0, 0).astype(LOW)
        d_up_ref[:, where] = mm(flip_ref[...], g_upward).astype(LOW)

    loop(hidden // tile, down_step)

    def up_back(step):
        where = cols(step, tile)
        wide_ref[:, where] = mm(g_up_ref[...], w_up_ref[where, :], 1, 1) + g_sum_ref[:, where]

    loop(tiles, up_back)

    def first_back(step):
        at = rows_at(step)
        g_normed = wide_ref[at, :]
        xhat = xhat_ref[at, :]
        add_to(gvec_ref, 3, column_sum(g_normed * xhat))
        add_to(gvec_ref, 4, column_sum(g_normed))
        g_hidden = norm_back(g_normed, xhat, inverse_ref[at, 0:1], gain_one)
        add_to(gvec_ref, 2, column_sum(g_hidden))
        g_hidden_ref[at, :] = g_hidden
        g_low_ref[at, :] = g_hidden.astype(LOW)

    loop(blocks, first_back)

    def out_back(step):
        where = cols(step, tile)
        g_ctx_ref[:, where] = mm(g_low_ref[...], w_out_ref[where, :], 1, 1)
        d_out_ref[where, :] = mm(ctx_low_ref[:, where], g_low_ref[...], 0, 0).astype(LOW)

    loop(tiles, out_back)


def plain_diagonals(diag_ref, out_ref, head):
    value = diag_ref[...]
    height = value.shape[0]
    while height > 1:
        height //= 2
        value = value[height:] + pltpu.roll(value[:height], height, axis=1)
    for k in range(8):
        out_ref[pl.ds(head * 8 + 7 - k, 1), :] = value[:, 128 * k : 128 * k + 128]


def attend_back(
    low_ref, rpe_ref, mask_ref, den_ref, ctx_ref, g_ctx_ref,
    g_feat_ref, g_low_ref, gvec_ref, grpe_ref,
    coef_ref, scores_ref, gk_ref, diag_ref, query_ref, key_ref, value_ref, num_ref,
):
    rows, breadth = ctx_ref.shape

    def pair_step(pair, carry):
        q_at = cols(pair, 128)
        k_at = pl.ds(pl.multiple_of(pair * 128 + breadth, 128), 128)
        v_at = pl.ds(pl.multiple_of(pair * 128 + 2 * breadth, 128), 128)
        lane = iota((128, 128), 1)
        ones = jnp.ones((128, 128), LOW)
        for side in range(2):
            coefficients(rpe_ref, pair * 2 + side, coef_ref)
            mine = lane >= 64 if side else lane < 64
            other = 0 if side else 64
            keep_half(low_ref, q_at, query_ref, side)
            keep_half(low_ref, k_at, key_ref, side)
            keep_half(low_ref, v_at, value_ref, side)
            diag_ref[...] = jnp.zeros_like(diag_ref)
            is_high, is_rest = lane == other, lane == other + 1
            extra = jnp.where(jnp.logical_or(is_high, is_rest), 1.0, 0.0)
            for block in range(rows // 128):
                at = slice(block * 128, block * 128 + 128)
                value_ref[at, :] = (value_ref[at, :].astype(F32) + extra).astype(LOW)
            for block in range(rows // 128):
                at = slice(block * 128, block * 128 + 128)
                kernel = mm(low_ref[at, q_at], key_ref[...], 1, 1)
                g_num = jnp.where(mine, g_ctx_ref[at, q_at] * (1.0 / den_ref[at, q_at]), 0.0)
                g_den = -mm2(g_num * ctx_ref[at, q_at], ones)
                num_ref[at, :] = g_num.astype(LOW)
                high = g_den.astype(LOW).astype(F32)
                extended = jnp.where(is_high, high, jnp.where(is_rest, g_den - high, g_num))
                g_scores = mm(extended.astype(LOW), value_ref[...], 1, 1)
                lead = 128 * (rows // 128 - 1 - block)
                weight = coef_ref[:, lead : lead + rows] * mask_ref[at, :]
                scores = kernel * weight
                g_kernel = (g_scores * weight).astype(LOW)
                diag_ref[:, lead : lead + rows] += g_scores * scores
                scores_ref[at, :] = scores.astype(LOW)
                gk_ref[at, :] = g_kernel
                g_query = mm(g_kernel, key_ref[...])
                if side:
                    g_query = g_query + g_feat_ref[at, q_at]
                g_feat_ref[at, q_at] = g_query
            g_key = mm(gk_ref[...], query_ref[...], 0, 0)
            g_value = mm(scores_ref[...], num_ref[...], 0, 0)
            if side:
                g_key = g_key + g_feat_ref[:, k_at]
                g_value = g_value + g_feat_ref[:, v_at]
            g_feat_ref[:, k_at] = g_key
            g_feat_ref[:, v_at] = g_value
            plain_diagonals(diag_ref, grpe_ref, pair * 2 + side)
        g_value = g_feat_ref[:, v_at]
        gvec_ref[0:1, v_at] = column_sum(g_value)
        g_low_ref[:, v_at] = g_value.astype(LOW)
        return carry

    lax.fori_loop(0, breadth // 128, pair_step, 0)
    flip = (jnp.where(iota((128, 128), 0) + iota((128, 128), 1) == 127, 1.0, 0.0)).astype(LOW)
    grpe_ref[...] = mm2(grpe_ref[...], flip)


def project_back(
    tokens_ref, w_ref, g_hidden_ref, phi_ref, scaled_ref, block_ref, ones_ref,
    g_feat_ref, g_low_ref, gvec_ref, g_tokens_ref, d_qkv_ref, flip_ref,
):
    breadth = tokens_ref.shape[1]
    tile = ones_ref.shape[0]
    per_part = breadth // tile
    scale = 64 ** (-0.25)

    def features(step, carry):
        where = cols(step, tile)
        upward = g_feat_ref[:, where] * phi_ref[:, where]
        total = mm2(upward, ones_ref[...])
        grad = mm2(upward, block_ref[lax.rem(step, per_part)], 1) - scaled_ref[:, where] * total
        grad = grad * scale
        gvec_ref[0:1, where] = column_sum(grad)
        g_low_ref[:, where] = grad.astype(LOW)
        return carry

    lax.fori_loop(0, 2 * per_part, features, 0)
    flip_ref[...] = jnp.transpose(tokens_ref[...])

    def weights(step, carry):
        where = cols(step, tile)
        d_qkv_ref[:, where] = mm(flip_ref[...], g_low_ref[:, where]).astype(LOW)
        return carry

    lax.fori_loop(0, 3 * per_part, weights, 0)

    def inputs(step, carry):
        where = cols(step, tile)
        g_tokens_ref[:, where] = mm(g_low_ref[...], w_ref[where, :], 1, 1) + g_hidden_ref[:, where]
        return carry

    lax.fori_loop(0, per_part, inputs, 0)


def backward_kernel(
    seq_ref, tokens_ref, feat_ref, w_ref, rpe_ref, scaled_ref, phi_ref, low_ref, den_ref, ctx_ref,
    g_ctx_ref, g_hidden_ref,
    g_tokens_ref, d_qkv_ref, gvec_ref, grpe_ref,
    mask_ref, block_ref, ones_ref, coef_ref, g_feat_ref, g_low_ref, scores_ref, gk_ref, diag_ref,
    query_ref, key_ref, value_ref, num_ref, flip_ref,
):
    build_tables(seq_ref, feat_ref, mask_ref, block_ref, ones_ref)
    gvec_ref[...] = jnp.zeros_like(gvec_ref)
    attend_back(
        low_ref, rpe_ref, mask_ref, den_ref, ctx_ref, g_ctx_ref, g_feat_ref, g_low_ref, gvec_ref, grpe_ref,
        coef_ref, scores_ref, gk_ref, diag_ref, query_ref, key_ref, value_ref, num_ref,
    )
    project_back(
        tokens_ref, w_ref, g_hidden_ref, phi_ref, scaled_ref, block_ref, ones_ref,
        g_feat_ref, g_low_ref, gvec_ref, g_tokens_ref, d_qkv_ref, flip_ref,
    )


def vmem(count):
    return [pl.BlockSpec(memory_space=pltpu.VMEM)] * count


def shape(dims, kind):
    return jax.ShapeDtypeStruct(dims, kind)


SCALARS = pl.BlockSpec(memory_space=pltpu.SMEM)


def forward_call(seq, tokens, feat, w_qkv, vec, rpe):
    rows, breadth = tokens.shape
    span = 2 * rows
    return pl.pallas_call(
        forward_kernel,
        out_shape=(
            shape((rows, 2 * breadth), F32), shape((rows, 2 * breadth), F32), shape((rows, 3 * breadth), LOW),
            shape((rows, breadth), F32), shape((rows, breadth), F32), shape((rows, breadth), LOW),
        ),
        in_specs=[SCALARS] + vmem(5),
        out_specs=tuple(vmem(6)),
        scratch_shapes=[
            pltpu.VMEM((rows, rows), F32), pltpu.VMEM((breadth // 256, 256, 256), LOW),
            pltpu.VMEM((256, 256), LOW), pltpu.VMEM((128, span), F32), pltpu.VMEM((rows, 128), LOW),
        ],
        compiler_params=pltpu.CompilerParams(vmem_limit_bytes=60 * MIB),
        name="attend",
    )(seq, tokens, feat, w_qkv, vec, rpe)


def middle_call(seq, tokens, cotangent, ctx_low, vec, w_out, w_up, w_down):
    rows, breadth = tokens.shape
    hidden = w_up.shape[1]
    return pl.pallas_call(
        middle_kernel,
        out_shape=(
            shape((rows, breadth), LOW), shape((rows, breadth), F32), shape((rows, breadth), F32),
            shape(w_out.shape, LOW), shape(w_up.shape, LOW), shape(w_down.shape, LOW), shape(vec.shape, F32),
        ),
        in_specs=[SCALARS] + vmem(7),
        out_specs=tuple(vmem(7)),
        scratch_shapes=[
            pltpu.VMEM((rows, breadth), F32), pltpu.VMEM((rows, breadth), F32), pltpu.VMEM((rows, breadth), LOW),
            pltpu.VMEM((rows, breadth), F32), pltpu.VMEM((rows, 128), F32), pltpu.VMEM((rows, hidden), LOW),
            pltpu.VMEM((rows, hidden), F32), pltpu.VMEM((rows, breadth), F32), pltpu.VMEM((rows, breadth), LOW),
            pltpu.VMEM((rows, hidden), LOW), pltpu.VMEM((breadth, rows), LOW),
        ],
        compiler_params=pltpu.CompilerParams(vmem_limit_bytes=60 * MIB),
        name="feed_forward",
    )(seq, tokens, cotangent, ctx_low, vec, w_out, w_up, w_down)


def backward_call(seq, tokens, feat, w_qkv, rpe, scaled, phi, low, den, ctx, g_ctx, g_hidden, vec):
    rows, breadth = tokens.shape
    span = 2 * rows
    return pl.pallas_call(
        backward_kernel,
        out_shape=(
            shape((rows, breadth), F32), shape(w_qkv.shape, LOW), shape(vec.shape, F32), shape(rpe.shape, F32),
        ),
        in_specs=[SCALARS] + vmem(11),
        out_specs=tuple(vmem(4)),
        scratch_shapes=[
            pltpu.VMEM((rows, rows), F32), pltpu.VMEM((breadth // 256, 256, 256), LOW),
            pltpu.VMEM((256, 256), LOW), pltpu.VMEM((128, span), F32), pltpu.VMEM((rows, 3 * breadth), F32),
            pltpu.VMEM((rows, 3 * breadth), LOW), pltpu.VMEM((rows, rows), LOW), pltpu.VMEM((rows, rows), LOW),
            pltpu.VMEM((128, span), F32), pltpu.VMEM((rows, 128), LOW), pltpu.VMEM((rows, 128), LOW),
            pltpu.VMEM((rows, 128), LOW), pltpu.VMEM((rows, 128), LOW), pltpu.VMEM((breadth, rows), LOW),
        ],
        compiler_params=pltpu.CompilerParams(vmem_limit_bytes=60 * MIB),
        name="attend_back",
    )(seq, tokens, feat, w_qkv, rpe, scaled, phi, low, den, ctx, g_ctx, g_hidden)


PIECE = 16
BLOCK_ROWS = 256


def place():
    me = lax.axis_index("dp")
    core = lax.rem(me, 2)
    x = lax.rem(me // 2, 2)
    y = lax.rem(me // 4, 2)
    z = me // 8
    first = x * (1 - core) + y * core
    second = y * (1 - core) + x * core
    return core, z, first, second


class Plane:
    def __init__(self, depth):
        self.depth = depth
        self.core, self.z, self.first, self.second = place()
        self.chip = self.at(self.z, self.first, self.second)
        self.sibling = self.chip * 2 + 1 - self.core
        self.over_first = self.device(self.z, 1 - self.first, self.second)
        self.over_second = self.device(self.z, self.first, 1 - self.second)

    def at(self, z, first, second):
        return 4 * z + first * (1 + self.core) + second * (2 - self.core)

    def device(self, z, first, second):
        return 2 * self.at(z, first, second) + self.core

    def spot(self, first, second):
        return first * (1 + self.core) + second * (2 - self.core)

    def ahead(self, distance):
        return lax.rem(self.z + distance, self.depth)

    def behind(self, distance):
        return lax.rem(self.z + self.depth - distance, self.depth)

    def greet(self):
        barrier = pltpu.get_barrier_semaphore()
        others = [self.sibling, self.over_first, self.over_second]
        others += [self.device(self.ahead(d), self.first, self.second) for d in range(1, self.depth)]
        for other in others:
            pl.semaphore_signal(barrier, inc=1, device_id=(other,), device_id_type=MESH)
        pl.semaphore_wait(barrier, len(others))


def remote(source, target, sems, item, slot, device):
    return pltpu.make_async_remote_copy(
        src_ref=source, dst_ref=target, send_sem=sems[0].at[item, slot], recv_sem=sems[1].at[item, slot],
        device_id=(device,), device_id_type=MESH,
    )


def each(count, step):
    def run(index, carry):
        step(index)
        return carry

    lax.fori_loop(0, count, run, 0)


def span(start, stop, step):
    def run(index, carry):
        step(index)
        return carry

    lax.fori_loop(start, stop, run, 0)


def half(ref, zs, spot, core):
    if len(ref.shape) == 5:
        return ref.at[zs, spot, core]
    breadth = ref.shape[3] // 2
    return ref.at[zs, spot, :, pl.ds(pl.multiple_of(core * breadth, 128), breadth)]


ALL = slice(None)


class Gather:
    def __init__(self, plane, full, sems):
        self.plane, self.full, self.sems = plane, full, sems
        self.here = plane.spot(plane.first, plane.second)
        self.across = plane.spot(1 - plane.first, plane.second)
        self.first_slot = plane.depth - 1
        self.second_slot = self.first_slot + 1
        self.core_slot = self.second_slot + 2

    def copy(self, item, zs, spot, slot, device, core=None):
        part = half(self.full[item], zs, spot, self.plane.core if core is None else core)
        return remote(part, part, self.sems, item, slot, device)

    def to_depth(self, item, distance):
        plane = self.plane
        target = plane.device(plane.ahead(distance), plane.first, plane.second)
        return self.copy(item, plane.z, self.here, distance - 1, target)

    def to_first(self, item):
        return self.copy(item, ALL, self.here, self.first_slot, self.plane.over_first)

    def to_second(self, item, first):
        spot = self.plane.spot(first, self.plane.second)
        return self.copy(item, ALL, spot, self.second_slot + first, self.plane.over_second)

    def to_core(self, item, spot):
        return self.copy(item, ALL, spot, self.core_slot + spot, self.plane.sibling)

    def begin(self, item):
        for distance in range(1, self.plane.depth):
            self.to_depth(item, distance).start()

    def over_depth(self, item):
        plane = self.plane
        for distance in range(1, plane.depth):
            self.copy(item, plane.behind(distance), self.here, distance - 1, plane.sibling).wait_recv()
        self.to_first(item).start()
        self.to_second(item, plane.first).start()
        self.to_core(item, self.here).start()

    def over_first(self, item):
        plane = self.plane
        self.copy(item, ALL, self.across, self.first_slot, plane.over_first).wait_recv()
        self.to_second(item, 1 - plane.first).start()
        self.to_core(item, self.across).start()

    def over_second(self, item):
        plane = self.plane
        for first in (plane.first, 1 - plane.first):
            spot = plane.spot(first, 1 - plane.second)
            self.copy(item, ALL, spot, self.second_slot + first, plane.over_second).wait_recv()
            self.to_core(item, spot).start()

    def over_core(self, item):
        plane = self.plane
        for spot in range(4):
            self.copy(item, ALL, spot, self.core_slot + spot, plane.sibling, 1 - plane.core).wait_recv()

    def sent(self, item):
        plane = self.plane
        for distance in range(1, plane.depth):
            self.to_depth(item, distance).wait_send()
        self.to_first(item).wait_send()
        for first in range(2):
            self.to_second(item, first).wait_send()
        for spot in range(4):
            self.to_core(item, spot).wait_send()


def one_hot(length, breadth):
    factor = (1 << 20) // length + 1
    col = iota((128, breadth), 1)
    owner = lax.shift_right_logical(col * factor, 20)
    return jnp.where(iota((128, breadth), 0) == col - owner * length, 1.0, 0.0).astype(LOW)


def owned(devices, length, breadth):
    factor = (1 << 20) // length + 1
    col = iota((devices, breadth), 1)
    return lax.shift_right_logical(col * factor, 20) == iota((devices, breadth), 0)


def pack_small(piece_refs, small_ref):
    small_ref[...] = jnp.zeros_like(small_ref)
    for row, piece in enumerate(piece_refs[:-1]):
        small_ref[row : row + 1, 0 : piece.shape[1]] = piece[...].astype(LOW).astype(F32)
    table = piece_refs[-1]
    for part in range(table.shape[1] // 128):
        row = len(piece_refs) - 1 + part
        small_ref[row : row + 1, :] = table[:, 128 * part : 128 * part + 128].astype(LOW).astype(F32)


def unpack_small(all_ref, lengths, table_rows, vec_ref, rpe_ref):
    devices = all_ref.shape[0] // PIECE
    vec_ref[...] = jnp.zeros_like(vec_ref)
    for row, length in enumerate(lengths):
        breadth = length * devices
        picked = all_ref[pl.ds(row, devices, stride=PIECE), :].astype(LOW)
        spread = jnp.where(owned(devices, length, breadth), mm(picked, one_hot(length, breadth)), 0.0)
        vec_ref[row : row + 1, 0:breadth] = column_sum(spread)
    for part in range(table_rows):
        rpe_ref[pl.ds(part, devices, stride=table_rows), :] = all_ref[
            pl.ds(len(lengths) + part, devices, stride=PIECE), :
        ]


ANYWHERE = pl.BlockSpec(memory_space=pl.ANY)


class Saver:
    def __init__(self, sources, targets, sems):
        self.copies = [
            pltpu.make_async_copy(source, target, sems.at[index])
            for index, (source, target) in enumerate(zip(sources, targets))
        ]

    def start(self, *indices):
        for index in indices:
            self.copies[index].start()

    def finish(self):
        for copy in self.copies:
            copy.wait()


def norm_forward(tokens_ref, wide_ref, vec_ref, xhat_ref, inverse_ref, normed_ref, normed_low_ref):
    rows, breadth = tokens_ref.shape
    gain, bias = vec_ref[3:4, :breadth], vec_ref[4:5, :breadth]

    def step(index):
        at = pl.ds(pl.multiple_of(index * 128, 128), 128)
        xhat, inverse = norm(tokens_ref[at, :].astype(F32) + wide_ref[at, :])
        xhat_ref[at, :] = xhat
        inverse_ref[at, :] = jnp.broadcast_to(inverse, (128, 128))
        normed = xhat * gain + bias
        normed_ref[at, :] = normed
        normed_low_ref[at, :] = normed.astype(LOW)

    each(rows // 128, step)


def norm_result(seq_ref, normed_ref, wide_ref, vec_ref, cot_ref, out_ref, g_sum_ref, gvec_ref):
    rows, breadth = normed_ref.shape
    gain, bias = vec_ref[6:7, :breadth], vec_ref[7:8, :breadth]
    valid_rows = seq_ref[0, 0] + seq_ref[0, 1]
    gvec_ref[...] = jnp.zeros_like(gvec_ref)

    def step(index):
        at = pl.ds(pl.multiple_of(index * 128, 128), 128)
        xhat, inverse = norm(normed_ref[at, :] + wide_ref[at, :])
        out_ref[at, :] = (xhat * gain + bias).astype(LOW)
        spot = iota((128, breadth), 0) + index * 128
        grad = jnp.where(spot < valid_rows, cot_ref[at, :].astype(F32), 0.0)
        add_to(gvec_ref, 6, column_sum(grad * xhat))
        add_to(gvec_ref, 7, column_sum(grad))
        g_sum = norm_back(grad, xhat, inverse, gain)
        add_to(gvec_ref, 5, column_sum(g_sum))
        g_sum_ref[at, :] = g_sum

    each(rows // 128, step)


def attend_pair(pair, q_at, k_at, v_at, low_ref, rpe_ref, mask_ref, den_ref, ctx_ref, ctx_low_ref, coef_ref, key_ref, score_ref, serve):
    rows = mask_ref.shape[0]
    tall = BLOCK_ROWS
    lower = iota((tall, 128), 1) < 64
    here = cols(pair, 128)
    for side in range(2):
        serve(pair, side)
        coefficients(rpe_ref, pair * 2 + side, coef_ref)
        keep_half(low_ref, k_at, key_ref, side)
        for block in range(rows // tall):
            at = slice(block * tall, block * tall + tall)
            kernel = mm(low_ref[at, q_at], key_ref[...], 1, 1)
            totals = []
            for part in range(tall // 128):
                start = block * tall + part * 128
                lead = rows - 128 - start
                weight = coef_ref[:, lead : lead + rows] * mask_ref[start : start + 128, :]
                scores = kernel[part * 128 : part * 128 + 128] * weight
                totals.append(jnp.sum(scores, axis=1, keepdims=True))
                score_ref[start : start + 128, :] = scores.astype(LOW)
            total = jnp.broadcast_to(jnp.concatenate(totals, axis=0), (tall, 128))
            context = mm(score_ref[at, :], low_ref[:, v_at]) * (1.0 / total)
            if side == 0:
                den_ref[at, here] = total
                ctx_ref[at, here] = context
            else:
                den_ref[at, here] = jnp.where(lower, den_ref[at, here], total)
                context = jnp.where(lower, ctx_ref[at, here], context)
                ctx_ref[at, here] = context
                ctx_low_ref[at, here] = context.astype(LOW)


def upward_tile(normed_low_ref, w, bias, act_ref, slope_ref, where):
    upward = mm(normed_low_ref[...], w[...]) + bias
    phi = 0.5 + 0.5 * lax.erf(upward * 0.5**0.5)
    density = jnp.exp(-0.5 * upward * upward) * 0.3989422804014327
    act_ref[:, where] = (upward * phi).astype(LOW)
    slope_ref[:, where] = phi + upward * density


def build_stack(feat_ref, stack_ref):
    tile = stack_ref.shape[2]
    head_size = feat_ref.shape[1]
    group = tile // head_size
    bits = head_size.bit_length() - 1
    same = lax.shift_right_logical(iota((tile, tile), 0), bits) == lax.shift_right_logical(iota((tile, tile), 1), bits)
    half = jnp.where(same, -0.5, 0.0).astype(LOW)
    for index in range(stack_ref.shape[0]):
        rows_of = []
        for inner in range(group):
            piece = feat_ref[index * group + inner].astype(F32)
            rows_of.append(jnp.concatenate([piece] * group, axis=1))
        full = jnp.where(same, jnp.concatenate(rows_of, axis=0), 0.0).astype(LOW)
        for part, value in enumerate((full, full, half, half)):
            stack_ref[index, part * tile : part * tile + tile, :] = value


def two_parts(value):
    high = value.astype(LOW)
    return [high, (value - high.astype(F32)).astype(LOW)]


def segment_mask(seq_ref, mask_ref):
    rows = mask_ref.shape[0]
    first_end = seq_ref[0, 0]
    second_end = first_end + seq_ref[0, 1]

    def segment(place):
        return (place >= first_end).astype(jnp.int32) + (place >= second_end).astype(jnp.int32)

    across = segment(iota((128, rows), 1))
    for start in range(0, rows, 128):
        down = segment(iota((128, rows), 0) + start)
        mask_ref[start : start + 128, :] = jnp.where(down == across, 1.0, 0.0)


def ahead_kernel(depth, pieces, *refs):
    seq_ref, tokens_ref, cot_ref, feat_ref, refs = refs[0], refs[1], refs[2], refs[3], refs[4:]
    matrices, refs = refs[:4], refs[4:]
    piece_refs, refs = refs[:pieces], refs[pieces:]
    out_ref, gvec_ref, vec_ref, rpe_ref, wide_ref, refs = refs[:5] + (refs[5:],)
    weights_hbm, kept_hbm, refs = refs[:4], refs[4:15], refs[15:]
    w_qkv, w_out, w_up, w_down, refs = refs[:4] + (refs[4:],)
    kept, refs = refs[:11], refs[11:]
    peers, refs = refs[:4], refs[4:]
    small_ref, all_ref, mask_ref, stack_ref, coef_ref, key_ref, score_ref, normed_ref = refs[:8]
    send, recv, peer_send, peer_recv, save_sem = refs[8:]
    scaled_ref, phi_ref, low_ref, den_ref, ctx_ref, ctx_low_ref = kept[:6]
    normed_low_ref, xhat_ref, inverse_ref, act_ref, slope_ref = kept[6:]
    rows, breadth = tokens_ref.shape
    groups, tile = w_qkv.shape[0], stack_ref.shape[2]
    up_tile, down_tile = w_up.shape[4], w_down.shape[4]

    plane = Plane(depth)
    core = plane.core
    pack_small(piece_refs, small_ref)
    thirds = range(groups)
    full = [all_ref] + [w_qkv.at[g] for g in thirds] + [w_out]
    full += [w_up.at[g] for g in thirds] + [w_down.at[g] for g in thirds]
    gather = Gather(plane, full, (send, recv))
    all_ref[plane.z, gather.here, core] = small_ref[...]
    plane.greet()
    swaps = [
        remote(matrix, peer, (peer_send, peer_recv), 0, index, plane.sibling)
        for index, (matrix, peer) in enumerate(zip(matrices, peers))
    ]
    for swap in swaps:
        swap.start()

    def assemble(item, matrix, starts, breadth_of):
        mine, other = matrices[matrix], peers[matrix]
        offset = core * (len(starts) * breadth_of)
        for number, start in enumerate(starts):
            at = pl.ds(pl.multiple_of(start, 128), breadth_of)
            own, peer = mine[:, at], other[:, at]
            both = jnp.concatenate([jnp.where(core == 0, own, peer), jnp.where(core == 0, peer, own)], axis=0)
            to = pl.ds(pl.multiple_of(offset + number * breadth_of, 128), breadth_of)
            full[item][plane.z, gather.here, :, to] = both.astype(LOW)

    def assemble_qkv(group):
        starts = []
        for number in range(3):
            place_of = 3 * core + number
            starts.append((place_of // 2) * breadth + group * tile + lax.rem(place_of, 2) * 128)
        assemble(1 + group, 0, starts, 128)

    flat_qkv = w_qkv.reshape(groups, breadth, 3 * tile)
    flat_out = w_out.reshape(breadth, breadth)
    flat_up = w_up.reshape(groups, breadth, up_tile)
    flat_down = w_down.reshape(groups, w_down.shape[1] * w_down.shape[2] * w_down.shape[3], down_tile)
    sources = [flat_qkv.at[g] for g in thirds] + [flat_out] + [flat_up.at[g] for g in thirds]
    sources += [flat_down.at[g] for g in thirds]
    targets = [weights_hbm[0].at[g] for g in thirds] + [weights_hbm[1]]
    targets += [weights_hbm[2].at[:, g * up_tile : g * up_tile + up_tile] for g in thirds]
    targets += [weights_hbm[3].at[:, g * down_tile : g * down_tile + down_tile] for g in thirds]
    saver = Saver(sources + list(kept), targets + list(kept_hbm), save_sem)
    first_kept = len(targets)

    def keep(*indices):
        saver.start(*[first_kept + index for index in indices])

    begin, along, first, second = gather.begin, gather.over_depth, gather.over_first, gather.over_second

    def whole(item):
        gather.over_core(item)
        if item:
            saver.start(item - 1)

    plan = {
        ("head", 1): ((second, 2), (along, 5)),
        ("head", 3): ((first, 4), (begin, 8), (whole, 2), (along, 6), (begin, 7)),
        ("project", 1): ((first, 5), (second, 3)),
        ("head", 5): ((second, 4),),
        ("project", 2): (
            (along, 7), (second, 5), (whole, 3), (begin, 9), (first, 6), (along, 8), (first, 7), (whole, 4),
        ),
        ("head", 8): ((whole, 5), (second, 6), (first, 8), (begin, 10)),
        ("head", 11): ((along, 9), (second, 7)),
        ("up", 0): ((second, 8), (first, 9), (whole, 6)),
        ("up", 2): ((first, 10), (whole, 8)),
        ("down", 0): ((second, 9),),
        ("down", 1): ((whole, 9), (second, 10)),
        ("down", 2): ((whole, 10),),
    }

    def serve(kind, index):
        for (work, number), steps in plan.items():
            if work == kind:

                @pl.when(index == number)
                def _(steps=steps):
                    for step, item in steps:
                        step(item)

    begin(0)
    swaps[0].wait_recv()
    assemble_qkv(0)
    begin(1)
    assemble_qkv(1)
    assemble_qkv(2)
    for swap in swaps[1:]:
        swap.wait_recv()
    assemble(4, 1, [core * (breadth // 2)], breadth // 2)
    for group in thirds:
        assemble(5 + group, 2, [group * up_tile + core * (up_tile // 2)], up_tile // 2)
        assemble(8 + group, 3, [group * down_tile + core * (down_tile // 2)], down_tile // 2)
    along(0)
    begin(2)
    segment_mask(seq_ref, mask_ref)
    first(0)
    along(1)
    second(0)
    along(2)
    begin(3)
    whole(0)
    begin(4)
    build_stack(feat_ref, stack_ref)
    first(1)
    along(3)
    first(2)
    begin(5)
    second(1)
    lengths = [piece.shape[1] for piece in piece_refs[:-1]]
    flat_all = all_ref.reshape(8 * depth * PIECE, 128)
    unpack_small(flat_all, lengths, piece_refs[-1].shape[1] // 128, vec_ref, rpe_ref)
    along(4)
    begin(6)
    whole(1)
    first(3)
    scale = 64 ** (-0.25)

    def serve_pair(pair, side):
        for (work, number), steps in plan.items():
            if work == "head" and number % 2 == side:

                @pl.when(pair == number // 2)
                def _(steps=steps):
                    for step, item in steps:
                        step(item)

    def group_step(group):
        serve("project", group)
        wide_ref[...] = mm(tokens_ref[...], flat_qkv[group])
        for part in range(3):
            where = pl.ds(pl.multiple_of(part * breadth + group * tile, tile), tile)
            value = wide_ref[:, part * tile : part * tile + tile] + vec_ref[0:1, where]
            if part < 2:
                scaled = value * scale
                scaled_ref[:, where] = scaled
                operand = jnp.concatenate(two_parts(scaled) + two_parts(scaled * scaled), axis=1)
                value = jnp.exp(mm(operand, stack_ref[group])) * 0.125
                phi_ref[:, where] = value
            low_ref[:, where] = value.astype(LOW)

        def pair_step(inner):
            pair = 2 * group + inner
            attend_pair(
                pair, cols(pair, 128), pl.ds(pl.multiple_of(pair * 128 + breadth, 128), 128),
                pl.ds(pl.multiple_of(pair * 128 + 2 * breadth, 128), 128),
                low_ref, rpe_ref, mask_ref, den_ref, ctx_ref, ctx_low_ref, coef_ref, key_ref, score_ref, serve_pair,
            )

        each(2, pair_step)

    each(groups, group_step)
    keep(0, 1, 2, 3, 4, 5)
    along(10)
    whole(7)
    wide_ref[...] = mm(ctx_low_ref[...], flat_out[...]) + vec_ref[2:3, :breadth]
    norm_forward(tokens_ref, wide_ref, vec_ref, xhat_ref, inverse_ref, normed_ref, normed_low_ref)
    keep(6, 7, 8)

    def upward_step(index):
        serve("up", index)
        where = cols(index, up_tile)
        upward_tile(normed_low_ref, flat_up.at[index], vec_ref[1:2, where], act_ref, slope_ref, where)

    each(groups, upward_step)
    keep(9, 10)

    def downward_step(index):
        serve("down", index)
        where = cols(index, down_tile)
        wide_ref[:, where] = mm(act_ref[...], flat_down[index]) + vec_ref[5:6, where]

    each(groups, downward_step)
    norm_result(seq_ref, normed_ref, wide_ref, vec_ref, cot_ref, out_ref, wide_ref, gvec_ref)
    for item in range(len(full)):
        gather.sent(item)
    for swap in swaps:
        swap.wait_send()
    saver.finish()


def ahead_call(depth, seq, tokens, cotangent, feat, matrices, pieces):
    rows, breadth = tokens.shape
    span_length = 2 * rows
    devices = 8 * depth
    groups, tile = 3, 256
    slots = depth - 1 + 1 + 2 + 4
    longest = max(piece.shape[1] for piece in pieces[:-1]) * devices
    table = pieces[-1].shape[1] * devices // 128
    w_qkv, w_out, w_up, w_down = matrices
    hidden = w_up.shape[1]
    lead = (depth, 4)
    full = [
        (groups,) + lead + (2 * w_qkv.shape[0], 3 * tile), lead + (2 * w_out.shape[0], breadth),
        (groups,) + lead + (2 * w_up.shape[0], hidden // groups),
        (groups,) + lead + (2 * w_down.shape[0], breadth // groups),
    ]
    saved = [(groups, breadth, 3 * tile), (breadth, breadth), (devices * w_up.shape[0], hidden), (devices * w_down.shape[0], breadth)]
    kept = [
        ((rows, 2 * breadth), F32), ((rows, 2 * breadth), F32), ((rows, 3 * breadth), LOW),
        ((rows, breadth), F32), ((rows, breadth), F32), ((rows, breadth), LOW),
        ((rows, breadth), LOW), ((rows, breadth), F32), ((rows, 128), F32), ((rows, hidden), LOW),
        ((rows, hidden), F32),
    ]
    items = 2 + 3 * groups
    return pl.pallas_call(
        functools.partial(ahead_kernel, depth, len(pieces)),
        out_shape=(
            shape((rows, breadth), LOW), shape((len(pieces) - 1, longest), F32),
            shape((len(pieces) - 1, longest), F32), shape((table, 128), F32), shape((rows, breadth), F32),
        )
        + tuple(shape(dims, LOW) for dims in saved)
        + tuple(shape(dims, kind) for dims, kind in kept),
        in_specs=[SCALARS] + vmem(3 + len(matrices) + len(pieces)),
        out_specs=tuple(vmem(5)) + (ANYWHERE,) * len(saved + kept),
        scratch_shapes=[pltpu.VMEM(dims, LOW) for dims in full]
        + [pltpu.VMEM(dims, kind) for dims, kind in kept]
        + [pltpu.VMEM(matrix.shape, F32) for matrix in matrices]
        + [
            pltpu.VMEM((PIECE, 128), F32), pltpu.VMEM((depth, 4, 2, PIECE, 128), F32),
            pltpu.VMEM((rows, rows), F32), pltpu.VMEM((groups, 4 * tile, tile), LOW),
            pltpu.VMEM((128, span_length), F32), pltpu.VMEM((rows, 128), LOW), pltpu.VMEM((rows, rows), LOW),
            pltpu.VMEM((rows, breadth), F32),
            pltpu.SemaphoreType.DMA((items, slots)), pltpu.SemaphoreType.DMA((items, slots)),
            pltpu.SemaphoreType.DMA((1, 4)), pltpu.SemaphoreType.DMA((1, 4)), pltpu.SemaphoreType.DMA((items - 1 + len(kept),)),
        ],
        compiler_params=pltpu.CompilerParams(
            collective_id=0, has_side_effects=True, vmem_limit_bytes=60 * MIB
        ),
        name="ahead",
    )(seq, tokens, cotangent, feat, *matrices, *pieces)


def prepare_back(group, slot, low_ref, den_ref, ctx_ref, g_ctx_ref, swap_ref, ext_ref, key_ref, val_ref, num_ref, flip_ref):
    rows = g_ctx_ref.shape[0]
    breadth = swap_ref.shape[0]
    where = cols(group, breadth)
    lane = jnp.bitwise_and(iota((128, breadth), 1), 127)
    lower = lane < 64

    def step(index):
        at = pl.ds(pl.multiple_of(index * 128, 128), 128)
        g_num = g_ctx_ref[at, where] * (1.0 / den_ref[slot, at, :])
        g_den = -mm2(g_num * ctx_ref[slot, at, :], swap_ref[...])
        high = g_den.astype(LOW).astype(F32)
        rest = g_den - high
        key = low_ref[slot, 1, at, :].astype(F32)
        value = low_ref[slot, 2, at, :].astype(F32)
        for side in range(2):
            mine = jnp.logical_not(lower) if side else lower
            other = 0 if side else 64
            is_high, is_rest = lane == other, lane == other + 1
            extended = jnp.where(mine, g_num, jnp.where(is_high, high, jnp.where(is_rest, rest, 0.0)))
            ext_ref[side, at, :] = extended.astype(LOW)
            key_ref[side, at, :] = jnp.where(mine, key, 0.0).astype(LOW)
            ones = jnp.where(jnp.logical_or(is_high, is_rest), 1.0, 0.0)
            val_ref[side, at, :] = jnp.where(mine, value, ones).astype(LOW)
        num_ref[at, :] = g_num.astype(LOW)

    each(rows // 128, step)
    flip_ref[0] = jnp.transpose(low_ref[slot, 0])
    flip_ref[1] = jnp.transpose(num_ref[...])


def attend_back_pair(
    pair, inner, slot, low_ref, rpe_ref, mask_ref, g_feat_ref, grpe_ref, coef_ref, scores_ref, gk_ref, diag_ref,
    ext_ref, key_ref, val_ref, flip_ref, turn_ref, serve,
):
    rows = mask_ref.shape[0]
    tall = BLOCK_ROWS
    here = cols(inner, 128)
    lower = iota((tall, 128), 1) < 64
    for side in range(2):
        serve(pair, side)
        coefficients(rpe_ref, pair * 2 + side, coef_ref)
        diag_ref[...] = jnp.zeros_like(diag_ref)
        for block in range(rows // tall):
            at = slice(block * tall, block * tall + tall)
            kernel = mm(low_ref[slot, 0, at, here], key_ref[side, :, here], 1, 1)
            g_scores = mm(ext_ref[side, at, here], val_ref[side, :, here], 1, 1)
            for part in range(tall // 128):
                start = block * tall + part * 128
                lead = rows - 128 - start
                inside = slice(part * 128, part * 128 + 128)
                weight = coef_ref[:, lead : lead + rows] * mask_ref[start : start + 128, :]
                scores = kernel[inside] * weight
                diag_ref[:, lead : lead + rows] += g_scores[inside] * scores
                scores_ref[start : start + 128, :] = scores.astype(LOW)
                gk_ref[start : start + 128, :] = (g_scores[inside] * weight).astype(LOW)
            g_query = mm(gk_ref[at, :], low_ref[slot, 1, :, here])
            if side:
                g_query = jnp.where(lower, g_feat_ref[at, here], g_query)
            g_feat_ref[at, here] = g_query
        head_rows = pl.ds(pl.multiple_of(inner * 128 + side * 64, 64), 64)
        turn_ref[0, head_rows, :] = mm(flip_ref[0, head_rows, :], gk_ref[...])
        turn_ref[1, head_rows, :] = mm(flip_ref[1, head_rows, :], scores_ref[...])
        diagonals(diag_ref, grpe_ref, pair * 2 + side)


def diagonals(diag_ref, out_ref, head):
    flip = jnp.where(iota((128, 128), 0) + iota((128, 128), 1) == 127, 1.0, 0.0).astype(LOW)
    value = diag_ref[...]
    high = value.astype(LOW)
    rest = (value - high.astype(F32)).astype(LOW)
    value = pltpu.roll(mm(flip, high) + mm(flip, rest), 0, axis=1, stride=1, stride_axis=0)
    sums = jnp.sum(value, axis=0, keepdims=True)
    for k in range(8):
        out_ref[pl.ds(head * 8 + 7 - k, 1), :] = sums[:, 128 * k : 128 * k + 128]


class Item:
    def __init__(self, given, buffers, row):
        self.given = given
        self.from_core, self.from_second, self.from_first, self.from_depth, self.leaving = buffers
        self.row = row


class Scatter:
    def __init__(self, plane, sems):
        self.plane, self.sems = plane, sems
        self.here = plane.spot(plane.first, plane.second)
        self.across = plane.spot(1 - plane.first, plane.second)
        self.first_slot = plane.depth - 1
        self.second_slot = self.first_slot + 1
        self.core_slot = self.second_slot + 2
        self.last_slot = self.core_slot + 1

    def with_core(self, item):
        return remote(
            half(item.given, ALL, ALL, 1 - self.plane.core), item.from_core, self.sems, item.row, self.core_slot,
            self.plane.sibling,
        )

    def begin(self, item):
        self.with_core(item).start()

    def to_second(self, item, first):
        spot = self.plane.spot(first, 1 - self.plane.second)
        return remote(
            half(item.given, ALL, spot, self.plane.core), item.from_second.at[first], self.sems, item.row,
            self.second_slot + first, self.plane.over_second,
        )

    def to_first(self, item):
        return remote(
            half(item.given, ALL, self.across, self.plane.core), item.from_first, self.sems, item.row,
            self.first_slot, self.plane.over_first,
        )

    def to_depth(self, item, distance):
        plane = self.plane
        z = plane.ahead(distance)
        return remote(
            half(item.given, z, self.here, plane.core), item.from_depth.at[distance - 1], self.sems, item.row,
            distance - 1, plane.device(z, plane.first, plane.second),
        )

    def join(self, item, spot, piece):
        def step(z):
            target = half(item.given, z, spot, self.plane.core)
            target[...] = target[...] + piece(z)

        each(self.plane.depth, step)

    def core(self, item):
        plane = self.plane
        self.with_core(item).wait_recv()
        for first in range(2):
            spot = plane.spot(first, 1 - plane.second)
            self.join(item, spot, lambda z, spot=spot: item.from_core[z, spot])
            self.to_second(item, first).start()
        for first in range(2):
            spot = plane.spot(first, plane.second)
            self.join(item, spot, lambda z, spot=spot: item.from_core[z, spot])

    def second(self, item):
        plane = self.plane
        away = 1 - plane.first
        self.to_second(item, away).wait_recv()
        self.join(item, self.across, lambda z: item.from_second[away, z])
        self.to_first(item).start()
        self.to_second(item, plane.first).wait_recv()
        self.join(item, self.here, lambda z: item.from_second[plane.first, z])

    def first(self, item):
        self.to_first(item).wait_recv()
        self.join(item, self.here, lambda z: item.from_first[z])
        for distance in range(1, self.plane.depth):
            self.to_depth(item, distance).start()

    def summed(self, item):
        plane = self.plane
        for distance in range(1, plane.depth):
            self.to_depth(item, distance).wait_recv()
        value = half(item.given, plane.z, self.here, plane.core)[...].astype(F32)
        for distance in range(1, plane.depth):
            value = value + item.from_depth[distance - 1].astype(F32)
        return value

    def columns(self, item, core):
        breadth = item.leaving.shape[1]
        return pl.ds(pl.multiple_of(core * breadth, 128), breadth)

    def last(self, item, target):
        core = self.plane.core
        return remote(
            item.leaving, target.at[:, self.columns(item, core)], self.sems, item.row, self.last_slot,
            self.plane.sibling,
        )

    def along(self, item, target):
        core = self.plane.core
        value = self.summed(item)
        height = value.shape[0] // 2
        upper, lower = value[:height], value[height:]
        target[:, self.columns(item, core)] = jnp.where(core == 0, upper, lower)
        item.leaving[...] = jnp.where(core == 0, lower, upper)
        self.last(item, target).start()

    def sent(self, item, target=None):
        self.with_core(item).wait_send()
        for first in range(2):
            self.to_second(item, first).wait_send()
        self.to_first(item).wait_send()
        for distance in range(1, self.plane.depth):
            self.to_depth(item, distance).wait_send()
        if target is not None:
            core = self.plane.core
            self.last(item, target).wait_send()
            arrived = target.at[:, self.columns(item, 1 - core)]
            remote(
                item.leaving, arrived, self.sems, item.row, self.last_slot, self.plane.sibling
            ).wait_recv()


def pack_grads(gvec_ref, lengths, grpe_ref, flat_ref):
    devices = flat_ref.shape[0] // PIECE
    table_rows = grpe_ref.shape[0] // devices
    flat_ref[...] = jnp.zeros_like(flat_ref)
    for row, length in enumerate(lengths):
        breadth = length * devices
        value = gvec_ref[row : row + 1, 0:breadth]
        spread = jnp.where(owned(devices, length, breadth), jnp.broadcast_to(value, (devices, breadth)), 0.0)
        flat_ref[pl.ds(row, devices, stride=PIECE), :] = mm2(spread, one_hot(length, breadth), 1)
    for part in range(table_rows):
        flat_ref[pl.ds(len(lengths) + part, devices, stride=PIECE), :] = grpe_ref[
            pl.ds(part, devices, stride=table_rows), :
        ]


def build_back(feat_ref, stack_ref):
    tile = stack_ref.shape[2]
    head_size = feat_ref.shape[1]
    group = tile // head_size
    bits = head_size.bit_length() - 1
    same = lax.shift_right_logical(iota((tile, tile), 0), bits) == lax.shift_right_logical(iota((tile, tile), 1), bits)
    last = stack_ref.shape[0] - 1
    for index in range(last):
        rows_of = []
        for inner in range(group):
            piece = jnp.transpose(feat_ref[index * group + inner].astype(F32))
            rows_of.append(jnp.concatenate([piece] * group, axis=1))
        full = jnp.where(same, jnp.concatenate(rows_of, axis=0), 0.0).astype(LOW)
        for part in range(2):
            stack_ref[index, part * tile : part * tile + tile, :] = full
    for part in range(2):
        stack_ref[last, part * tile : part * tile + tile, :] = jnp.where(same, 1.0, 0.0).astype(LOW)


def build_swap(swap_ref):
    tile = swap_ref.shape[0]
    down = lax.shift_right_logical(iota((tile, tile), 0), 6)
    across = lax.shift_right_logical(iota((tile, tile), 1), 6)
    swap_ref[...] = jnp.where(jnp.bitwise_xor(down, 1) == across, 1.0, 0.0).astype(LOW)


def behind_kernel(depth, lengths, *refs):
    seq_ref, feat_ref, vec_ref, rpe_ref, gvec_in_ref, g_sum_ref, refs = refs[:6] + (refs[6:],)
    w_qkv_hbm, w_out_hbm, w_up_hbm, w_down_hbm, refs = refs[:4] + (refs[4:],)
    scaled_hbm, phi_hbm, low_hbm, den_hbm, ctx_hbm, ctx_low_hbm, refs = refs[:6] + (refs[6:],)
    normed_low_hbm, xhat_hbm, inverse_hbm, act_hbm, slope_hbm, tokens_hbm, refs = refs[:6] + (refs[6:],)
    g_tokens_hbm, s_qkv, s_out, s_up, s_down, s_small, refs = refs[:6] + (refs[6:],)
    d_qkv, d_out, d_up, d_down, d_small, refs = refs[:5] + (refs[5:],)
    buffers, refs = [refs[5 * index : 5 * index + 5] for index in range(5)], refs[25:]
    g_hidden_ref, g_ctx_ref, g_low_ref, gvec_ref, grpe_ref, g_qkv_ref, refs = refs[:6] + (refs[6:],)
    send, recv, load_sem = refs
    rows, breadth = g_sum_ref.shape
    hidden = w_up_hbm.shape[1]
    tile, height = 256, 128
    wide = min(768, breadth)
    plane = Plane(depth)
    scatter = Scatter(plane, (send, recv))
    down, up, out = [
        Item(given, buffers[index], 2 - index)
        for given, index in ((d_down, 2), (d_up, 1), (d_out, 0))
    ]
    small = Item(d_small, buffers[4], 3)
    flat_down, flat_up, flat_out, flat_qkv = d_down.reshape(hidden, breadth), d_up.reshape(breadth, hidden), (
        d_out.reshape(breadth, breadth)
    ), d_qkv.reshape(breadth // tile, breadth, 3 * tile)
    flat_small = d_small.reshape(8 * depth * PIECE, 128)

    def qkv(group):
        return Item(d_qkv.at[group], [buffer.at[group] for buffer in buffers[3]], 4 + group)

    def load(source, target, index):
        return pltpu.make_async_copy(source, target, load_sem.at[index])

    def feed_forward(
        w_out_ref, w_up_ref, w_down_ref, act_ref, slope_ref, normed_low_ref, flip_ref,
        inverse_ref, ctx_low_ref,
    ):
        chunk = slope_ref.shape[2]
        chunks = hidden // chunk
        pending = {}

        def columns(index):
            return slice(index * chunk, index * chunk + chunk)

        acts = [
            load(act_hbm.at[:, columns(index)], act_ref.at[:, columns(index)], 2 * chunks + index)
            for index in range(chunks)
        ]

        def fetch(index):
            at = columns(index)
            pending[index] = [
                load(w_down_hbm.at[at, :], w_down_ref.at[at, :], 2 * index),
                load(slope_hbm.at[:, at], slope_ref.at[index % 2], 2 * index + 1),
            ]
            for copy in pending[index]:
                copy.start()

        for copy in acts:
            copy.start()
        fetch(0)
        fetch(1)
        base = 3 * chunks
        later = [
            load(normed_low_hbm, normed_low_ref, base), load(w_up_hbm, w_up_ref, base + 1),
            load(xhat_hbm, g_hidden_ref, base + 2), load(inverse_hbm, inverse_ref, base + 3),
            load(w_out_hbm, w_out_ref, base + 4), load(ctx_low_hbm, ctx_low_ref, base + 5),
        ]
        g_low_ref[...] = g_sum_ref[...].astype(LOW)
        gvec_ref[...] = gvec_in_ref[...]
        plane.greet()
        for index in range(chunks):
            acts[index].wait()

            at = columns(index)
            flat_down[at, :] = mm(act_ref[:, at], g_low_ref[...], 0, 0).astype(LOW)
        scatter.begin(down)
        for index in range(chunks):
            for copy in pending[index]:
                copy.wait()
            if index == 2:
                scatter.core(down)

            at = columns(index)
            g_upward = mm(g_low_ref[...], w_down_ref[at, :], 1, 1) * slope_ref[index % 2]
            gvec_ref[1:2, at] = column_sum(g_upward)
            act_ref[:, at] = g_upward.astype(LOW)
            if index + 2 < chunks:
                fetch(index + 2)
            if index == 0:
                for copy in later:
                    copy.start()
        for copy in later:
            copy.wait()
        flip_ref[...] = jnp.transpose(normed_low_ref[...])

        def up_step(step):
            where = cols(step, wide)
            flat_up[:, where] = mm(flip_ref[...], act_ref[:, where]).astype(LOW)

        each(hidden // wide, up_step)
        scatter.begin(up)

        g_sum_ref[...] = mm(act_ref[...], w_up_ref[...], 1, 1) + g_sum_ref[...]
        gain_one = vec_ref[3:4, :breadth]

        def first_back(step):
            at = pl.ds(pl.multiple_of(step * height, height), height)
            g_normed = g_sum_ref[at, :]
            xhat = g_hidden_ref[at, :]
            add_to(gvec_ref, 3, column_sum(g_normed * xhat))
            add_to(gvec_ref, 4, column_sum(g_normed))
            g_hidden = norm_back(g_normed, xhat, inverse_ref[at, 0:1], gain_one)
            add_to(gvec_ref, 2, column_sum(g_hidden))
            g_hidden_ref[at, :] = g_hidden
            g_low_ref[at, :] = g_hidden.astype(LOW)

        each(rows // height, first_back)

        flat_out[...] = mm(ctx_low_ref[...], g_low_ref[...], 0, 0).astype(LOW)
        scatter.begin(out)
        scatter.core(up)
        scatter.second(down)
        g_ctx_ref[...] = mm(g_low_ref[...], w_out_ref[...], 1, 1)

    chunk = min(768, hidden)
    pl.run_scoped(
        feed_forward,
        pltpu.VMEM(w_out_hbm.shape, LOW), pltpu.VMEM(w_up_hbm.shape, LOW), pltpu.VMEM(w_down_hbm.shape, LOW),
        pltpu.VMEM((rows, hidden), LOW), pltpu.VMEM((2, rows, chunk), F32),
        pltpu.VMEM((rows, breadth), LOW), pltpu.VMEM((breadth, rows), LOW),
        pltpu.VMEM((rows, 128), F32), pltpu.VMEM((rows, breadth), LOW),
    )

    calls = {
        4: (lambda: scatter.core(out), lambda: scatter.first(down)),
        7: (lambda: scatter.second(up),),
        9: (lambda: scatter.core(qkv(0)), lambda: scatter.first(up)),
        11: (lambda: scatter.second(out), lambda: scatter.core(qkv(1))),
    }

    def serve(pair, side):
        for head, steps in calls.items():
            if head % 2 == side:

                @pl.when(pair == head // 2)
                def _(steps=steps):
                    for step in steps:
                        step()

    def attention(
        w_qkv_ref, flip_ref, scaled_ref, phi_ref, low_ref, den_ref, ctx_ref, g_feat_ref, coef_ref,
        scores_ref, gk_ref, diag_ref, ext_ref, key_ref, val_ref, num_ref, turn_low_ref, turn_ref, swap_ref, mask_ref, stack_ref,
    ):
        groups = breadth // tile

        def part(ref, at, number):
            return ref.at[:, pl.ds(pl.multiple_of(at * tile + number * breadth, tile), tile)]

        def loads(group):
            slot = lax.rem(group, 2)
            copies = []
            for number in range(3):
                copies.append((part(low_hbm, group, number), low_ref.at[slot, number]))
            copies.append((part(den_hbm, group, 0), den_ref.at[slot]))
            copies.append((part(ctx_hbm, group, 0), ctx_ref.at[slot]))
            for number in range(2):
                copies.append((part(scaled_hbm, group, number), scaled_ref.at[slot, number]))
                copies.append((part(phi_hbm, group, number), phi_ref.at[slot, number]))
            return [
                load(source, target, slot * 9 + index) for index, (source, target) in enumerate(copies)
            ]

        base = 18
        tokens_copy = load(tokens_hbm, g_low_ref, base)

        def weights(group):
            return load(w_qkv_hbm.at[group], w_qkv_ref.at[group % 2], base + 1 + group)

        for copy in loads(0):
            copy.start()
        for copy in (tokens_copy, weights(0), weights(1)):
            copy.start()
        segment_mask(seq_ref, mask_ref)
        build_back(feat_ref, stack_ref)
        tokens_copy.wait()
        flip_ref[...] = jnp.transpose(g_low_ref[...])
        build_swap(swap_ref)
        scale = 64 ** (-0.25)

        def group_step(group):
            slot = lax.rem(group, 2)
            for copy in loads(group):
                copy.wait()

            @pl.when(group + 1 < groups)
            def _():
                for copy in loads(group + 1):
                    copy.start()

            prepare_back(
                group, slot, low_ref, den_ref, ctx_ref, g_ctx_ref, swap_ref, ext_ref, key_ref, val_ref, num_ref,
                turn_low_ref,
            )

            def pair_step(inner):
                pair = 2 * group + inner
                attend_back_pair(
                    pair, inner, slot, low_ref, rpe_ref, mask_ref, g_feat_ref, grpe_ref, coef_ref, scores_ref,
                    gk_ref, diag_ref, ext_ref, key_ref, val_ref, turn_low_ref, turn_ref, serve,
                )

            each(2, pair_step)

            g_feat_ref[:, tile : 2 * tile] = jnp.transpose(turn_ref[0])
            g_feat_ref[:, 2 * tile : 3 * tile] = jnp.transpose(turn_ref[1])
            for number in range(3):
                at = slice(number * tile, number * tile + tile)
                where = pl.ds(pl.multiple_of(group * tile + number * breadth, tile), tile)
                grad = g_feat_ref[:, at]
                if number < 2:
                    upward = jnp.concatenate(two_parts(grad * phi_ref[slot, number]), axis=1)
                    total = mm(upward, stack_ref[groups])
                    grad = mm(upward, stack_ref[group]) - scaled_ref[slot, number] * total
                    grad = grad * scale
                gvec_ref[0:1, where] = column_sum(grad)
                g_qkv_ref[group, :, at] = grad.astype(LOW)
            flat_qkv[group] = mm(flip_ref[...], g_qkv_ref[group]).astype(LOW)
            scatter.begin(qkv(group))

        each(groups, group_step)
        scatter.second(qkv(0))
        scatter.core(qkv(2))
        scatter.along(down, s_down)
        scatter.first(out)
        scatter.first(qkv(0))
        flip = jnp.where(iota((128, 128), 0) + iota((128, 128), 1) == 127, 1.0, 0.0).astype(LOW)
        grpe_ref[...] = mm2(grpe_ref[...], flip)
        pack_grads(gvec_ref, lengths, grpe_ref, flat_small)
        scatter.begin(small)
        scatter.second(qkv(1))

        def inputs(group):
            weights(group).wait()
            g_hidden_ref[...] += mm(g_qkv_ref[group], w_qkv_ref[group % 2], 1, 1)
            if group + 2 < groups:
                weights(group + 2).start()

        inputs(0)
        inputs(1)
        scatter.core(small)
        inputs(2)

    pl.run_scoped(
        attention,
        pltpu.VMEM((2,) + w_qkv_hbm.shape[1:], LOW), pltpu.VMEM((breadth, rows), LOW),
        pltpu.VMEM((2, 2, rows, tile), F32), pltpu.VMEM((2, 2, rows, tile), F32),
        pltpu.VMEM((2, 3, rows, tile), LOW), pltpu.VMEM((2, rows, tile), F32), pltpu.VMEM((2, rows, tile), F32),
        pltpu.VMEM((rows, 3 * tile), F32), pltpu.VMEM((128, 2 * rows), F32), pltpu.VMEM((rows, rows), LOW),
        pltpu.VMEM((rows, rows), LOW), pltpu.VMEM((128, 2 * rows), F32), pltpu.VMEM((2, rows, tile), LOW),
        pltpu.VMEM((2, rows, tile), LOW), pltpu.VMEM((2, rows, tile), LOW), pltpu.VMEM((rows, tile), LOW),
        pltpu.VMEM((2, tile, rows), LOW), pltpu.VMEM((2, tile, rows), F32), pltpu.VMEM((tile, tile), LOW),
        pltpu.VMEM((rows, rows), F32), pltpu.VMEM((breadth // tile + 1, 2 * tile, tile), LOW),
    )
    result = load(g_hidden_ref, g_tokens_hbm, 31)
    result.start()
    scatter.second(qkv(2))
    scatter.first(qkv(1))
    scatter.second(small)
    scatter.along(out, s_out)
    scatter.along(up, s_up)
    scatter.first(small)
    scatter.first(qkv(2))
    scatter.along(qkv(1), s_qkv.at[1])
    scatter.along(qkv(0), s_qkv.at[0])
    scatter.along(qkv(2), s_qkv.at[2])
    s_small[...] = scatter.summed(small)
    for item, target in ((down, s_down), (up, s_up), (out, s_out), (small, None)):
        scatter.sent(item, target)
    for group in range(breadth // tile):
        scatter.sent(qkv(group), s_qkv.at[group])
    result.wait()


def behind_call(depth, seq, feat, vec, rpe, gvec, g_sum, weights, kept, tokens, lengths):
    rows, breadth = tokens.shape
    chips = 4 * depth
    devices = 2 * chips
    w_qkv, w_out, w_up, w_down = weights
    group = 3 * 256
    groups = w_qkv.shape[0]
    table = rpe.shape[0]
    blocks = [(w.shape[0] // devices, w.shape[1]) for w in (w_out, w_up, w_down)]
    lead = (depth, 4)
    given = [lead + (2 * block[0], block[1]) for block in blocks]
    qkv_block = (w_qkv.shape[1] // devices, group)

    def buffers(block, kind, front=()):
        if kind == LOW:
            part, leaving = (2 * block[0], block[1] // 2), (block[0], block[1] // 2)
        else:
            part, leaving = block, (8, 128)
        numbers = [lead, (2, depth), (depth,), (depth - 1,)]
        return [pltpu.VMEM(front + number + part, kind) for number in numbers] + [pltpu.VMEM(front + leaving, F32)]

    slots = depth - 1 + 1 + 2 + 2
    scratch = [pltpu.VMEM((groups,) + lead + (2 * qkv_block[0], group), LOW)]
    scratch += [pltpu.VMEM(dims, LOW) for dims in given]
    scratch += [pltpu.VMEM(lead + (2, PIECE, 128), F32)]
    for block in blocks:
        scratch += buffers(block, LOW)
    scratch += buffers(qkv_block, LOW, (groups,)) + buffers((PIECE, 128), F32)
    scratch += [
        pltpu.VMEM((rows, breadth), F32), pltpu.VMEM((rows, breadth), F32), pltpu.VMEM((rows, breadth), LOW),
        pltpu.VMEM(vec.shape, F32), pltpu.VMEM((table, 128), F32), pltpu.VMEM((groups, rows, group), LOW),
        pltpu.SemaphoreType.DMA((7, slots)), pltpu.SemaphoreType.DMA((7, slots)), pltpu.SemaphoreType.DMA((32,)),
    ]
    return pl.pallas_call(
        functools.partial(behind_kernel, depth, lengths),
        out_shape=(
            shape((rows, breadth), F32), shape((groups,) + qkv_block, F32),
        ) + tuple(shape(block, F32) for block in blocks) + (shape((PIECE, 128), F32),),
        in_specs=[SCALARS] + vmem(5) + [ANYWHERE] * (4 + len(kept) + 1),
        out_specs=(ANYWHERE,) + tuple(vmem(5)),
        scratch_shapes=scratch,
        compiler_params=pltpu.CompilerParams(
            collective_id=1, has_side_effects=True, vmem_limit_bytes=62 * MIB
        ),
        name="behind",
    )(seq, feat, vec, rpe, gvec, g_sum, *weights, *kept, tokens)


def emit_kernel(count, lengths, *refs):
    big, small, refs = refs[:count], refs[count], refs[count + 1 :]
    outs, refs = refs[:count], refs[count:]
    pieces, held, sems = refs[: len(lengths) + 1], refs[len(lengths) + 1 : -1], refs[-1]
    inward = []
    for index in range(count):
        if len(big[index].shape) == 3:
            groups, _, breadth = big[index].shape
            tile = breadth // 3
            for group in range(groups):
                for part in range(3):
                    start = part * breadth + group * tile
                    source = big[index].at[group, :, part * tile : part * tile + tile]
                    inward.append((source, held[index].at[:, start : start + tile]))
        else:
            inward.append((big[index], held[index]))
    inward = [
        pltpu.make_async_copy(source, target, sems.at[0, index]) for index, (source, target) in enumerate(inward)
    ]
    outward = [pltpu.make_async_copy(held[index], outs[index], sems.at[1, index]) for index in range(count)]
    for copy in inward:
        copy.start()
    for row, length in enumerate(lengths):
        pieces[row][...] = small[row : row + 1, 0:length]
    table = pieces[-1]
    for part in range(table.shape[1] // 128):
        row = len(lengths) + part
        table[:, 128 * part : 128 * part + 128] = small[row : row + 1, :]
    for copy in inward:
        copy.wait()
    for copy in outward:
        copy.start()
    for copy in outward:
        copy.wait()


def emit_call(arrays, small, lengths, table):
    shapes = [
        (array.shape[1], array.shape[0] * array.shape[2]) if len(array.shape) == 3 else array.shape for array in arrays
    ]
    result = pl.pallas_call(
        functools.partial(emit_kernel, len(arrays), lengths),
        out_shape=tuple(shape(dims, array.dtype) for dims, array in zip(shapes, arrays))
        + tuple(shape((1, length), F32) for length in lengths + (table,)),
        in_specs=[ANYWHERE] * len(arrays) + vmem(1),
        out_specs=(ANYWHERE,) * len(arrays) + tuple(vmem(len(lengths) + 1)),
        scratch_shapes=[pltpu.VMEM(dims, array.dtype) for dims, array in zip(shapes, arrays)]
        + [pltpu.SemaphoreType.DMA((2, len(arrays) + 8))],
        compiler_params=pltpu.CompilerParams(vmem_limit_bytes=60 * MIB),
        name="emit",
    )(*arrays, small)
    return result[: len(arrays)], [piece.reshape(-1) for piece in result[len(arrays) :]]


def plain_gather(value):
    return lax.all_gather(value.astype(LOW), "dp", axis=0, tiled=True)


def plain_scatter(value):
    return lax.psum_scatter(value.astype(F32), "dp", scatter_dimension=0, tiled=True)


def body(
    depth, tokens, cotangent, seq_lengths, random_feat, w_qkv, b_qkv, w_out, b_out, ln1_gain, ln1_bias,
    w_up, b_up, w_down, b_down, ln2_gain, ln2_bias, rpe_table,
):
    vectors = (b_qkv, b_up, b_out, ln1_gain, ln1_bias, b_down, ln2_gain, ln2_bias)
    matrices = (w_qkv, w_out, w_up, w_down)
    lengths = tuple(piece.shape[0] for piece in vectors)
    if depth:
        pieces = [piece.reshape(1, -1) for piece in vectors + (rpe_table,)]
        result = ahead_call(depth, seq_lengths, tokens, cotangent, random_feat, matrices, pieces)
        out, gvec, vec, rpe = result[:4]
        g_sum, weights, kept = result[4], result[5:9], result[9:]
        g_tokens, s_qkv, s_out, s_up, s_down, small = behind_call(
            depth, seq_lengths, random_feat, vec, rpe, gvec, g_sum, weights, kept, tokens, lengths
        )
        arrays, pieces = emit_call(
            (out, g_tokens, s_qkv, s_out, s_up, s_down), small, lengths, rpe_table.shape[0]
        )
        out, g_tokens, s_qkv, s_out, s_up, s_down = arrays
    else:
        full_vectors = [plain_gather(piece).astype(F32) for piece in vectors]
        longest = max(piece.shape[0] for piece in full_vectors)
        vec = jnp.stack([jnp.pad(piece, (0, longest - piece.shape[0])) for piece in full_vectors])
        rpe = plain_gather(rpe_table).astype(F32).reshape(-1, 128)
        full_qkv, full_out, full_up, full_down = [plain_gather(piece) for piece in matrices]
        scaled, phi, low, den, ctx, ctx_low = forward_call(seq_lengths, tokens, random_feat, full_qkv, vec, rpe)
        out, g_hidden, g_ctx, d_out, d_up, d_down, gvec_one = middle_call(
            seq_lengths, tokens, cotangent, ctx_low, vec, full_out, full_up, full_down
        )
        g_tokens, d_qkv, gvec_two, grpe = backward_call(
            seq_lengths, tokens, random_feat, full_qkv, rpe, scaled, phi, low, den, ctx, g_ctx, g_hidden, vec
        )
        gvec = gvec_one + gvec_two
        s_qkv, s_out, s_up, s_down = [plain_scatter(grad) for grad in (d_qkv, d_out, d_up, d_down)]
        devices = lax.axis_size("dp")
        pieces = [plain_scatter(gvec[row, : length * devices]) for row, length in enumerate(lengths)]
        pieces.append(plain_scatter(grpe.reshape(-1)))
    p_qkv, p_up, p_out, p_gain_one, p_bias_one, p_down, p_gain_two, p_bias_two, p_rpe = pieces
    return (
        out, g_tokens, s_qkv, p_qkv, s_out, p_out, p_gain_one, p_bias_one, s_up, p_up, s_down, p_down,
        p_gain_two, p_bias_two, p_rpe,
    )


def solution(mesh):
    wide, flat = P("dp", None), P("dp")
    devices = mesh.shape["dp"]
    depth = devices // 8 if devices == 32 else 0
    in_specs = (
        wide, wide, wide, P(), wide, flat, wide, flat, flat, flat, wide, flat, wide, flat, flat, flat, flat,
    )
    out_specs = (
        wide, wide, wide, flat, wide, flat, flat, flat, wide, flat, wide, flat, flat, flat, flat,
    )
    return jax.shard_map(
        functools.partial(body, depth), mesh=mesh, in_specs=in_specs, out_specs=out_specs, check_vma=False
    )
```

profile of v0, /device:TPU:0, one launch (start us, length us, event | category | flops | bytes accessed | tf_op | source)
XLA Modules:
  0.0 178.1 jit_solution(11442921449348276472)
XLA Ops:
  0.6 1.2 reshape.92.refs_16_
  1.9 79.9 %ahead.1 = (bf16[512,768]{1,0:T(8,128)(2,1)}, f32[8,3072]{1,0:T(8,128)}, f32[8,3072]{1,0:T(8,128)}, f32[96,128]{1,0:T(8,128)}, f32[512,768]{1,0:T(8,128)}, /*ind...) custom-call(s32[1,2]{1,0:T(1,128)} %refs_0_.3, ...), custom_call_target="tpu_custom_call" | custom-call | tf_op jit(solution)/shard_map/ahead/pallas_call | solution.py:1038
  81.8 89.9 %behind.1 = (f32[512,768]{1,0:T(8,128)}, f32[3,24,768]{2,1,0:T(8,128)}, f32[24,768]{1,0:T(8,128)}, f32[24,3072]{1,0:T(8,128)}, f32[96,768]{1,0:T(8,128)}, /*index=5*/f32[16,128]{1,0:T(8,128)}) custom-call(s32[1,2]{1,0:T(1,128)} %refs_0_.3, bf16[12,64,64]{2,1,0:T(8,128)(2,1)} %refs_1_.3, f32[8,3072]{1,0:T(8,128)} %get-tuple-element.57.refs_2_, ...), custom_call_target="tpu_custom_call" | custom-call | tf_op jit(solution)/shard_map/behind/pallas_call | solution.py:1625
  171.7 5.2 %emit.1 = (bf16[512,768]{1,0:T(8,128)(2,1)}, f32[512,768]{1,0:T(8,128)}, f32[24,2304]{1,0:T(8,128)}, f32[24,768]{1,0:T(8,128)}, f32[24,3072]{1,0:T(8,128)}, /*in...) custom-call(bf16[512,768]{1,0:T(8,128)(2,1)} %get-tuple-element.56.r, ...), custom_call_target="tpu_custom_call" | custom-call | tf_op jit(solution)/shard_map/emit/pallas_call | solution.py:1680
  176.9 1.3 reduce
where the time goes:
time: 178 us
  Pallas kernels  175 us (98%)
    pallas_call x1, Pallas kernels, behind_call(): pl.pallas_call(functools.partial(behind_kernel, depth, lengths), out_shap...  89.9 us
    pallas_call x1, Pallas kernels, ahead_call(): pl.pallas_call(functools.partial(ahead_kernel, depth, len(pieces)), out_s...  79.9 us
    pallas_call x1, Pallas kernels, emit_call(): pl.pallas_call(functools.partial(emit_kernel, len(arrays), lengths), out_...  5.15 us

commit v1 on v0

--- a/solution.py
+++ b/solution.py
@@ -662,9 +662,10 @@
     for row, piece in enumerate(piece_refs[:-1]):
         small_ref[row : row + 1, 0 : piece.shape[1]] = piece[...].astype(LOW).astype(F32)
     table = piece_refs[-1]
-    for part in range(table.shape[1] // 128):
+    for part in range(table.shape[0] // 128):
         row = len(piece_refs) - 1 + part
-        small_ref[row : row + 1, :] = table[:, 128 * part : 128 * part + 128].astype(LOW).astype(F32)
+        value = table[128 * part : 128 * part + 128].reshape(1, 128)
+        small_ref[row : row + 1, :] = value.astype(LOW).astype(F32)
 
 
 def unpack_small(all_ref, lengths, table_rows, vec_ref, rpe_ref):
@@ -941,7 +942,7 @@
     second(1)
     lengths = [piece.shape[1] for piece in piece_refs[:-1]]
     flat_all = all_ref.reshape(8 * depth * PIECE, 128)
-    unpack_small(flat_all, lengths, piece_refs[-1].shape[1] // 128, vec_ref, rpe_ref)
+    unpack_small(flat_all, lengths, piece_refs[-1].shape[0] // 128, vec_ref, rpe_ref)
     along(4)
     begin(6)
     whole(1)
@@ -1018,7 +1019,7 @@
     groups, tile = 3, 256
     slots = depth - 1 + 1 + 2 + 4
     longest = max(piece.shape[1] for piece in pieces[:-1]) * devices
-    table = pieces[-1].shape[1] * devices // 128
+    table = pieces[-1].shape[0] * devices // 128
     w_qkv, w_out, w_up, w_down = matrices
     hidden = w_up.shape[1]
     lead = (depth, 4)
@@ -1641,7 +1642,7 @@
     big, small, refs = refs[:count], refs[count], refs[count + 1 :]
     outs, refs = refs[:count], refs[count:]
     pieces, held, sems = refs[: len(lengths) + 1], refs[len(lengths) + 1 : -1], refs[-1]
-    inward = []
+    inward, owners = [], []
     for index in range(count):
         if len(big[index].shape) == 3:
             groups, _, breadth = big[index].shape
@@ -1651,8 +1652,10 @@
                     start = part * breadth + group * tile
                     source = big[index].at[group, :, part * tile : part * tile + tile]
                     inward.append((source, held[index].at[:, start : start + tile]))
+                    owners.append(index)
         else:
             inward.append((big[index], held[index]))
+            owners.append(index)
     inward = [
         pltpu.make_async_copy(source, target, sems.at[0, index]) for index, (source, target) in enumerate(inward)
     ]
@@ -1662,13 +1665,14 @@
     for row, length in enumerate(lengths):
         pieces[row][...] = small[row : row + 1, 0:length]
     table = pieces[-1]
-    for part in range(table.shape[1] // 128):
+    for part in range(table.shape[0] // 128):
         row = len(lengths) + part
-        table[:, 128 * part : 128 * part + 128] = small[row : row + 1, :]
-    for copy in inward:
-        copy.wait()
-    for copy in outward:
-        copy.start()
+        table[128 * part : 128 * part + 128] = small[row : row + 1, :].reshape(128)
+    for index in range(count):
+        for owner, copy in zip(owners, inward):
+            if owner == index:
+                copy.wait()
+        outward[index].start()
     for copy in outward:
         copy.wait()
 
@@ -1680,7 +1684,7 @@
     result = pl.pallas_call(
         functools.partial(emit_kernel, len(arrays), lengths),
         out_shape=tuple(shape(dims, array.dtype) for dims, array in zip(shapes, arrays))
-        + tuple(shape((1, length), F32) for length in lengths + (table,)),
+        + tuple(shape((1, length), F32) for length in lengths) + (shape((table,), F32),),
         in_specs=[ANYWHERE] * len(arrays) + vmem(1),
         out_specs=(ANYWHERE,) * len(arrays) + tuple(vmem(len(lengths) + 1)),
         scratch_shapes=[pltpu.VMEM(dims, array.dtype) for dims, array in zip(shapes, arrays)]
@@ -1707,7 +1711,7 @@
     matrices = (w_qkv, w_out, w_up, w_down)
     lengths = tuple(piece.shape[0] for piece in vectors)
     if depth:
-        pieces = [piece.reshape(1, -1) for piece in vectors + (rpe_table,)]
+        pieces = [piece.reshape(1, -1) for piece in vectors] + [rpe_table]
         result = ahead_call(depth, seq_lengths, tokens, cotangent, random_feat, matrices, pieces)
         out, gvec, vec, rpe = result[:4]
         g_sum, weights, kept = result[4], result[5:9], result[9:]

time: 178 us -> 176 us (0.989)
  no operation moved by 1% of the time
where the time goes in v1:
time: 176 us; the launch traced here: 175 us
  Pallas kernels  174 us (99%)
    pallas_call x1, Pallas kernels, behind_call(): pl.pallas_call(functools.partial(behind_kernel, depth, lengths), out_shap...  89.9 us
    pallas_call x1, Pallas kernels, ahead_call(): pl.pallas_call(functools.partial(ahead_kernel, depth, len(pieces)), out_s...  79.9 us
    pallas_call x1, Pallas kernels, emit_call(): pl.pallas_call(functools.partial(emit_kernel, len(arrays), lengths), out_...  4.63 us

profile of v1, /device:TPU:0, one launch (start us, length us, event | category | flops | bytes accessed | tf_op | source)
XLA Modules:
  0.0 175.3 jit_solution(15037259035283849242)
XLA Ops:
  0.7 79.9 %ahead.1 = (bf16[512,768]{1,0:T(8,128)(2,1)}, f32[8,3072]{1,0:T(8,128)}, f32[8,3072]{1,0:T(8,128)}, f32[96,128]{1,0:T(8,128)}, f32[512,768]{1,0:T(8,128)}, /*ind...) custom-call(s32[1,2]{1,0:T(1,128)} %refs_0_.3, ...), custom_call_target="tpu_custom_call" | custom-call | tf_op jit(solution)/shard_map/ahead/pallas_call | solution.py:1039
  80.6 89.9 %behind.1 = (f32[512,768]{1,0:T(8,128)}, f32[3,24,768]{2,1,0:T(8,128)}, f32[24,768]{1,0:T(8,128)}, f32[24,3072]{1,0:T(8,128)}, f32[96,768]{1,0:T(8,128)}, /*index=5*/f32[16,128]{1,0:T(8,128)}) custom-call(s32[1,2]{1,0:T(1,128)} %refs_0_.3, bf16[12,64,64]{2,1,0:T(8,128)(2,1)} %refs_1_.3, f32[8,3072]{1,0:T(8,128)} %get-tuple-element.57.refs_2_, ...), custom_call_target="tpu_custom_call" | custom-call | tf_op jit(solution)/shard_map/behind/pallas_call | solution.py:1626
  170.5 4.6 %emit.1 = (bf16[512,768]{1,0:T(8,128)(2,1)}, f32[512,768]{1,0:T(8,128)}, f32[24,2304]{1,0:T(8,128)}, f32[24,768]{1,0:T(8,128)}, f32[24,3072]{1,0:T(8,128)}, /*in...) custom-call(bf16[512,768]{1,0:T(8,128)(2,1)} %get-tuple-element.56.r, ...), custom_call_target="tpu_custom_call" | custom-call | tf_op jit(solution)/shard_map/emit/pallas_call | solution.py:1684

commit v2 on v1

--- a/solution.py
+++ b/solution.py
@@ -1639,9 +1639,17 @@
 
 
 def emit_kernel(count, lengths, *refs):
-    big, small, refs = refs[:count], refs[count], refs[count + 1 :]
+    big, small_hbm, refs = refs[:count], refs[count], refs[count + 1 :]
     outs, refs = refs[:count], refs[count:]
-    pieces, held, sems = refs[: len(lengths) + 1], refs[len(lengths) + 1 : -1], refs[-1]
+    number = len(lengths) + 1
+    targets, refs = refs[:number], refs[number:]
+    held, pieces, small, sems, piece_sems = refs[:count], refs[count : count + number], refs[-3], refs[-2], refs[-1]
+    arrive = pltpu.make_async_copy(small_hbm, small, piece_sems.at[number])
+    arrive.start()
+    leave = [
+        pltpu.make_async_copy(piece, target, piece_sems.at[index])
+        for index, (piece, target) in enumerate(zip(pieces, targets))
+    ]
     inward, owners = [], []
     for index in range(count):
         if len(big[index].shape) == 3:
@@ -1662,18 +1670,21 @@
     outward = [pltpu.make_async_copy(held[index], outs[index], sems.at[1, index]) for index in range(count)]
     for copy in inward:
         copy.start()
+    arrive.wait()
     for row, length in enumerate(lengths):
         pieces[row][...] = small[row : row + 1, 0:length]
     table = pieces[-1]
     for part in range(table.shape[0] // 128):
         row = len(lengths) + part
         table[128 * part : 128 * part + 128] = small[row : row + 1, :].reshape(128)
+    for copy in leave:
+        copy.start()
     for index in range(count):
         for owner, copy in zip(owners, inward):
             if owner == index:
                 copy.wait()
         outward[index].start()
-    for copy in outward:
+    for copy in outward + leave:
         copy.wait()
 
 
@@ -1685,10 +1696,14 @@
         functools.partial(emit_kernel, len(arrays), lengths),
         out_shape=tuple(shape(dims, array.dtype) for dims, array in zip(shapes, arrays))
         + tuple(shape((1, length), F32) for length in lengths) + (shape((table,), F32),),
-        in_specs=[ANYWHERE] * len(arrays) + vmem(1),
-        out_specs=(ANYWHERE,) * len(arrays) + tuple(vmem(len(lengths) + 1)),
+        in_specs=[ANYWHERE] * (len(arrays) + 1),
+        out_specs=(ANYWHERE,) * (len(arrays) + len(lengths) + 1),
         scratch_shapes=[pltpu.VMEM(dims, array.dtype) for dims, array in zip(shapes, arrays)]
-        + [pltpu.SemaphoreType.DMA((2, len(arrays) + 8))],
+        + [pltpu.VMEM((1, length), F32) for length in lengths]
+        + [
+            pltpu.VMEM((table,), F32), pltpu.VMEM(small.shape, F32), pltpu.SemaphoreType.DMA((2, len(arrays) + 8)),
+            pltpu.SemaphoreType.DMA((len(lengths) + 2,)),
+        ],
         compiler_params=pltpu.CompilerParams(vmem_limit_bytes=60 * MIB),
         name="emit",
     )(*arrays, small)

time: 176 us -> 175 us (level)
  no operation moved by 1% of the time
where the time goes in v2:
time: 175 us; the launch traced here: 174 us
  Pallas kernels  174 us (99%)
    pallas_call x1, Pallas kernels, behind_call(): pl.pallas_call(functools.partial(behind_kernel, depth, lengths), out_shap...  89.9 us
    pallas_call x1, Pallas kernels, ahead_call(): pl.pallas_call(functools.partial(ahead_kernel, depth, len(pieces)), out_s...  79.9 us
    pallas_call x1, Pallas kernels, emit_call(): pl.pallas_call(functools.partial(emit_kernel, len(arrays), lengths), out_...  3.73 us

profile of v2, /device:TPU:0, one launch (start us, length us, event | category | flops | bytes accessed | tf_op | source)
XLA Modules:
  0.0 174.4 jit_solution(16762324531958943885)
XLA Ops:
  0.7 79.9 %ahead.1 = (bf16[512,768]{1,0:T(8,128)(2,1)}, f32[8,3072]{1,0:T(8,128)}, f32[8,3072]{1,0:T(8,128)}, f32[96,128]{1,0:T(8,128)}, f32[512,768]{1,0:T(8,128)}, /*ind...) custom-call(s32[1,2]{1,0:T(1,128)} %refs_0_.3, ...), custom_call_target="tpu_custom_call" | custom-call | tf_op jit(solution)/shard_map/ahead/pallas_call | solution.py:1039
  80.6 89.9 %behind.1 = (f32[512,768]{1,0:T(8,128)}, f32[3,24,768]{2,1,0:T(8,128)}, f32[24,768]{1,0:T(8,128)}, f32[24,3072]{1,0:T(8,128)}, f32[96,768]{1,0:T(8,128)}, /*index=5*/f32[16,128]{1,0:T(8,128)}) custom-call(s32[1,2]{1,0:T(1,128)} %refs_0_.3, bf16[12,64,64]{2,1,0:T(8,128)(2,1)} %refs_1_.3, f32[8,3072]{1,0:T(8,128)} %get-tuple-element.57.refs_2_, ...), custom_call_target="tpu_custom_call" | custom-call | tf_op jit(solution)/shard_map/behind/pallas_call | solution.py:1626
  170.5 3.7 %emit.1 = (bf16[512,768]{1,0:T(8,128)(2,1)}, f32[512,768]{1,0:T(8,128)}, f32[24,2304]{1,0:T(8,128)}, f32[24,768]{1,0:T(8,128)}, f32[24,3072]{1,0:T(8,128)}, /*in...) custom-call(bf16[512,768]{1,0:T(8,128)(2,1)} %get-tuple-element.56.r, ...), custom_call_target="tpu_custom_call" | custom-call | tf_op jit(solution)/shard_map/emit/pallas_call | solution.py:1695

commit v3 on v2

--- a/solution.py
+++ b/solution.py
@@ -898,9 +898,9 @@
         ("head", 11): ((along, 9), (second, 7)),
         ("up", 0): ((second, 8), (first, 9), (whole, 6)),
         ("up", 2): ((first, 10), (whole, 8)),
-        ("down", 0): ((second, 9),),
-        ("down", 1): ((whole, 9), (second, 10)),
-        ("down", 2): ((whole, 10),),
+        ("down", 0): ((second, 9),) + tuple((gather.sent, item) for item in range(6)),
+        ("down", 1): ((whole, 9), (second, 10), (gather.sent, 6), (gather.sent, 7)),
+        ("down", 2): ((gather.sent, 8), (gather.sent, 9), (whole, 10)),
     }
 
     def serve(kind, index):
@@ -920,6 +920,8 @@
     assemble_qkv(2)
     for swap in swaps[1:]:
         swap.wait_recv()
+    for swap in swaps:
+        swap.wait_send()
     assemble(4, 1, [core * (breadth // 2)], breadth // 2)
     for group in thirds:
         assemble(5 + group, 2, [group * up_tile + core * (up_tile // 2)], up_tile // 2)
@@ -1005,10 +1007,7 @@
 
     each(groups, downward_step)
     norm_result(seq_ref, normed_ref, wide_ref, vec_ref, cot_ref, out_ref, wide_ref, gvec_ref)
-    for item in range(len(full)):
-        gather.sent(item)
-    for swap in swaps:
-        swap.wait_send()
+    gather.sent(len(full) - 1)
     saver.finish()
 
 
@@ -1579,12 +1578,14 @@
     scatter.along(up, s_up)
     scatter.first(small)
     scatter.first(qkv(2))
+    scatter.sent(down, s_down)
     scatter.along(qkv(1), s_qkv.at[1])
     scatter.along(qkv(0), s_qkv.at[0])
+    scatter.sent(up, s_up)
+    scatter.sent(out, s_out)
     scatter.along(qkv(2), s_qkv.at[2])
     s_small[...] = scatter.summed(small)
-    for item, target in ((down, s_down), (up, s_up), (out, s_out), (small, None)):
-        scatter.sent(item, target)
+    scatter.sent(small)
     for group in range(breadth // tile):
         scatter.sent(qkv(group), s_qkv.at[group])
     result.wait()

time: 175 us -> 174 us (level)
  no operation moved by 1% of the time
where the time goes in v3:
time: 174 us
  Pallas kernels  173 us (99%)
    pallas_call x1, Pallas kernels, behind_call(): pl.pallas_call(functools.partial(behind_kernel, depth, lengths), out_shap...  89.7 us
    pallas_call x1, Pallas kernels, ahead_call(): pl.pallas_call(functools.partial(ahead_kernel, depth, len(pieces)), out_s...  79.9 us
    pallas_call x1, Pallas kernels, emit_call(): pl.pallas_call(functools.partial(emit_kernel, len(arrays), lengths), out_...  3.73 us

profile of v3, /device:TPU:0, one launch (start us, length us, event | category | flops | bytes accessed | tf_op | source)
XLA Modules:
  0.0 174.1 jit_solution(5258128455839025011)
XLA Ops:
  0.7 79.9 %ahead.1 = (bf16[512,768]{1,0:T(8,128)(2,1)}, f32[8,3072]{1,0:T(8,128)}, f32[8,3072]{1,0:T(8,128)}, f32[96,128]{1,0:T(8,128)}, f32[512,768]{1,0:T(8,128)}, /*ind...) custom-call(s32[1,2]{1,0:T(1,128)} %refs_0_.3, ...), custom_call_target="tpu_custom_call" | custom-call | tf_op jit(solution)/shard_map/ahead/pallas_call | solution.py:1038
  80.6 89.7 %behind.1 = (f32[512,768]{1,0:T(8,128)}, f32[3,24,768]{2,1,0:T(8,128)}, f32[24,768]{1,0:T(8,128)}, f32[24,3072]{1,0:T(8,128)}, f32[96,768]{1,0:T(8,128)}, /*index=5*/f32[16,128]{1,0:T(8,128)}) custom-call(s32[1,2]{1,0:T(1,128)} %refs_0_.3, bf16[12,64,64]{2,1,0:T(8,128)(2,1)} %refs_1_.3, f32[8,3072]{1,0:T(8,128)} %get-tuple-element.57.refs_2_, ...), custom_call_target="tpu_custom_call" | custom-call | tf_op jit(solution)/shard_map/behind/pallas_call | solution.py:1627
  170.2 3.7 %emit.1 = (bf16[512,768]{1,0:T(8,128)(2,1)}, f32[512,768]{1,0:T(8,128)}, f32[24,2304]{1,0:T(8,128)}, f32[24,768]{1,0:T(8,128)}, f32[24,3072]{1,0:T(8,128)}, /*in...) custom-call(bf16[512,768]{1,0:T(8,128)(2,1)} %get-tuple-element.56.r, ...), custom_call_target="tpu_custom_call" | custom-call | tf_op jit(solution)/shard_map/emit/pallas_call | solution.py:1696
